TPU v7x, 768 devices: a whole 4x8x12 slice. The times are simulated.
768 devices in a mesh: grp: 96 (over y_lo, z, x), fsdp: 8 (over y_hi, core).
Axes of the slice: x: 4, y: 8 (y_hi: 4, y_lo: 2; y = y_hi * 2 + y_lo), z: 12, core: 2. Of those that a mesh axis runs over, the one named last changes fastest.
Arguments:
- text: bfloat16 [98304, 8192], P(('grp', 'fsdp'))
- vision: bfloat16 [12288, 8192], P(('grp', 'fsdp'))
- vision_token: int32 [12288], P(('grp', 'fsdp')), may hold values from 0 to 98303, as said below
- gain: bfloat16 [8192], P('fsdp'), may hold values from 0.099609375 to 1.8984375
- cotangent: bfloat16 [98304, 8192], P(('grp', 'fsdp')), may hold values from -6 to 6
Outputs:
- vision_grad: bfloat16 [12288, 8192], P(('grp', 'fsdp'))
- gain_grad: float32 [8192], P('fsdp')
Inputs may be any that keep to these rules, and one draw needn't show every extreme that they name: `vision_token`: device d of the flattened grp+fsdp order holds vision rows d * 16 to (d + 1) * 16 - 1 and token rows d * 128 to (d + 1) * 128 - 1. The rows held in group g go to tokens of group (g + 24) mod 96; a device sends at most 4 rows to any one device, and in every group some device receives exactly 4 rows from every device of its source group. No token receives two rows.
All inputs are finite; a program needn't handle non-finite values.
Results may differ from a plain program's by a relative error of at most 0.001.
Values may be sent and summed in bfloat16 or wider, within the bound.
No kernel may reach another device: no remote copies, remote signals or barrier semaphores. Data moves between devices by JAX's collectives and lax.ppermute only.
A program may use at most 32 MiB of HBM per device.

v0:
```python
import jax
import jax.numpy as jnp
from jax import lax
from jax.sharding import PartitionSpec as P


def shifted(value, axis, steps):
    count = lax.axis_size(axis)
    pairs = [(source, (source + steps) % count) for source in range(count)]
    return lax.ppermute(value, axis, pairs)


def slot_order(target, groups, capacity):
    onehot = (target[:, None] == jnp.arange(groups)[None, :]).astype(jnp.int32)
    rank = jnp.sum((jnp.cumsum(onehot, axis=0) - 1) * onehot, axis=1)
    return target * capacity + rank


def pack_rows(rows, local, target, groups, capacity, tok_dev):
    slot = slot_order(target, groups, capacity)
    buffer = jnp.zeros((groups * capacity, rows.shape[1]), rows.dtype).at[slot].set(rows)
    places = jnp.full((groups * capacity,), tok_dev, jnp.int32).at[slot].set(local)
    return (buffer.reshape(groups, capacity, rows.shape[1]), places.reshape(groups, capacity), slot)


def norm_backward(values, upper, full_gain):
    inv = lax.rsqrt(jnp.mean(values * values, axis=-1, keepdims=True) + 1e-06)
    scaled = upper * full_gain
    inner = jnp.mean(values * scaled, axis=-1, keepdims=True)
    token_grad = (inv * scaled - values * inv * inv * inv * inner).astype(jnp.bfloat16)
    return (token_grad, upper * values * inv)


def shards(text, vision, vision_token, gain, cotangent):
    groups = lax.axis_size("fsdp")
    hop = lax.axis_size("grp") // 4
    tok_dev, width = text.shape
    capacity = vision.shape[0] // 4
    local = vision_token % tok_dev
    target = vision_token // tok_dev % groups
    full_gain = lax.all_gather(gain, "fsdp", axis=0, tiled=True).astype(jnp.float32)
    buffer, places, slot = pack_rows(vision, local, target, groups, capacity, tok_dev)
    spread, spread_places = (
        lax.all_to_all(buffer, "fsdp", split_axis=0, concat_axis=0, tiled=True),
        lax.all_to_all(places, "fsdp", split_axis=0, concat_axis=0, tiled=True),
    )
    arrived, arrived_places = shifted((spread, spread_places), "grp", hop)
    arrived = arrived.reshape(groups * capacity, width)
    arrived_places = arrived_places.reshape(groups * capacity)
    assembled = text.at[arrived_places].set(arrived, mode="drop")
    token_grad, term_rows = norm_backward(
        assembled.astype(jnp.float32), cotangent.astype(jnp.float32), full_gain
    )
    terms = jnp.sum(term_rows, axis=0)
    picked = jnp.take(token_grad, jnp.minimum(arrived_places, tok_dev - 1), axis=0)
    picked = picked.reshape(groups, capacity, width)
    hopped = shifted(picked, "grp", -hop)
    returned = lax.all_to_all(hopped, "fsdp", split_axis=0, concat_axis=0, tiled=True).reshape(
        groups * capacity, width
    )
    vision_grad = returned[slot]
    share_width = width // groups
    total = lax.psum(terms, ("grp", "fsdp"))
    gain_grad = lax.dynamic_slice_in_dim(total, lax.axis_index("fsdp") * share_width, share_width)
    return (vision_grad, gain_grad)


def solution(mesh):
    return jax.shard_map(
        shards,
        mesh=mesh,
        in_specs=(
            P(("grp", "fsdp"), None),
            P(("grp", "fsdp"), None),
            P(("grp", "fsdp")),
            P("fsdp"),
            P(("grp", "fsdp"), None),
        ),
        out_specs=(P(("grp", "fsdp"), None), P("fsdp")),
        check_vma=False,
    )
```

profile of v0, /device:TPU:1, one launch (start us, length us, event | category | flops | bytes accessed | tf_op | source)
XLA Modules:
  0.0 279.2 jit_solution(8615464659485805712)
XLA Ops:
  0.6 0.0 copy-start.3
  0.6 0.6 copy-done.3
  1.3 0.0 copy-start.2
  1.3 0.0 copy-start
  1.3 0.1 fusion.12
  1.4 0.2 select_reduce_fusion
  1.6 0.6 scatter_custom_fusion
  2.2 0.7 all_to_all.14
  2.9 13.7 %all-to-all-start = ((s32[8,1,4]{2,1,0:T(1,128)}), s32[8,1,4]{2,1,0:T(1,128)S(1)}, u32[]{:S(2)}, u32[]{:S(2)}) async-start(s32[8,1,4]{2,1,0:T(1,128)} %bitcast), calls=%async_computation | async-start | bytes 8192 | tf_op jit(solution)/shard_map/all_to_all | solution.py:45
  16.6 1.5 scatter_custom_fusion.1
  18.2 1.0 reshape.94
  19.1 4.4 %all-to-all-done = s32[8,1,4]{2,1,0:T(1,128)S(1)} async-done(((s32[8,1,4]{2,1,0:T(1,128)}), s32[8,1,4]{2,1,0:T(1,128)S(1)}, u32[]{:S(2)}, u32[]{:S(2)}) %all-to-all-start) | async-done | bytes 160 | tf_op jit(solution)/shard_map/all_to_all | solution.py:45
  23.6 4.1 %all-to-all-start.1 = ((bf16[8,4,8192]{2,1,0:T(4,128)(2,1)}), bf16[8,4,8192]{2,1,0:T(4,128)(2,1)S(1)}, u32[]{:S(2)}, u32[]{:S(2)}) async-start(bf16[8,4,8192]{2,1,0:T(4,128)(2,1)} %reshape.94), calls=%async_computation.1 | async-start | bytes 1048576 | tf_op jit(solution)/shard_map/all_to_all | solution.py:44
  27.7 0.0 copy-done.2
  27.7 20.8 %all_gather.3 = bf16[8192]{0:T(1024)(128)(2,1)S(1)} all-gather(bf16[1024]{0:T(1024)(128)(2,1)S(1)} %copy-done.2), channel_id=1, replica_groups=mesh['grp'=96,'fsdp'=8] {'fsdp'}, dimensions={0}, use_global_device_ids=true | all-gather | bytes 18432 | tf_op jit(solution)/shard_map/all_gather | solution.py:41
  48.4 0.1 copy.14
  48.5 12.5 %collective-permute-start = (s32[8,4]{0,1:T(4,128)S(1)}, s32[8,4]{0,1:T(4,128)S(1)}, u32[]{:S(2)}, u32[]{:S(2)}) collective-permute-start(s32[8,4]{0,1:T(4,128)S(1)} %bitcast.6), channel_id=1, source_target_pairs={{0,192},{8,200},{16,208},{24,216},{32,224},{40,232},{48,240},{56,2... | collective-permute-start | bytes 392 | tf_op jit(solution)/shard_map/ppermute | solution.py:10
  61.0 1.2 collective-permute-done
  62.2 0.1 copy.16
  62.3 0.1 reshape.93
  62.4 0.0 all-to-all-done.1
  62.4 9.4 %collective-permute-start.1 = (bf16[8,4,8192]{2,1,0:T(4,128)(2,1)S(1)}, bf16[8,4,8192]{2,1,0:T(4,128)(2,1)S(1)}, u32[]{:S(2)}, u32[]{:S(2)}) collective-permute-start(bf16[8,4,8192]{2,1,0:T(4,128)(2,1)S(1)} %all-to-all-done.1), channel_id=1, source_target_pairs={{0,192},{8,200},{16,208},{24,216},{32,224},{40,232},{48,240},{56,2... | collective-permute-start | bytes 1572872 | tf_op jit(solution)/shard_map/ppermute | solution.py:10
  71.8 0.1 copy.15
  71.9 13.4 %collective-permute-done.1 = bf16[8,4,8192]{2,1,0:T(4,128)(2,1)S(1)} collective-permute-done((bf16[8,4,8192]{2,1,0:T(4,128)(2,1)S(1)}, bf16[8,4,8192]{2,1,0:T(4,128)(2,1)S(1)}, u32[]{:S(2)}, u32[]{:S(2)}) %collective-permute-start.1) | collective-permute-done | bytes 524320 | tf_op jit(solution)/shard_map/ppermute | solution.py:10
  85.3 0.1 reshape.133
  85.4 0.0 copy-done
  85.4 2.5 scatter_fusion
  87.9 0.0 copy-start.1
  87.9 0.5 fusion.3
  88.4 1.1 copy-done.1
  89.5 1.8 fusion.9
  91.3 2.7 fusion.2
  94.1 3.2 %gather_fusion = bf16[32,8192]{1,0:T(8,128)(2,1)S(1)} fusion(bf16[128,8192]{1,0:T(8,128)(2,1)} %fusion.2, s32[1024]{0:T(1024)S(1)} %pad_clamp_fusion.1), kind=kCustom, calls=%fused_computation | custom fusion | bytes 1048704 | tf_op jit(solution)/shard_map/jit(_take)/gather | solution.py:55
  97.3 0.2 gather.10
  97.5 0.3 broadcast_select_fusion
  97.8 10.0 %collective-permute-start.2 = (bf16[8,4,8192]{2,1,0:T(4,128)(2,1)S(1)}, bf16[8,4,8192]{2,1,0:T(4,128)(2,1)}, u32[]{:S(2)}, u32[]{:S(2)}) collective-permute-start(bf16[8,4,8192]{2,1,0:T(4,128)(2,1)S(1)} %broadcast_select_fusion), channel_id=1, source_target_pairs={{0,576},{8,584},{16,592},{24,600},{32,608},{40,616},{48,624},{56,6... | collective-permute-start | bytes 1572872 | tf_op jit(solution)/shard_map/ppermute | solution.py:10
  107.8 17.1 %collective-permute-done.2 = bf16[8,4,8192]{2,1,0:T(4,128)(2,1)} collective-permute-done((bf16[8,4,8192]{2,1,0:T(4,128)(2,1)S(1)}, bf16[8,4,8192]{2,1,0:T(4,128)(2,1)}, u32[]{:S(2)}, u32[]{:S(2)}) %collective-permute-start.2) | collective-permute-done | bytes 524320 | tf_op jit(solution)/shard_map/ppermute | solution.py:10
  124.9 5.4 %all-to-all-start.2 = ((bf16[8,4,8192]{2,1,0:T(4,128)(2,1)}), bf16[8,4,8192]{2,1,0:T(4,128)(2,1)S(1)}, u32[]{:S(2)}, u32[]{:S(2)}) async-start(bf16[8,4,8192]{2,1,0:T(4,128)(2,1)} %collective-permute-done.2), calls=%async_computation.2 | async-start | bytes 1048576 | tf_op jit(solution)/shard_map/all_to_all | solution.py:58
  130.3 146.7 %psum.7 = f32[8192]{0:T(1024)S(1)} all-reduce(f32[8192]{0:T(1024)S(1)} %get-tuple-element.2), channel_id=1, replica_groups=mesh['grp'=96,'fsdp'=8] {'grp','fsdp'}, use_global_device_ids=true, to_apply=%region_8.9 | all-reduce | flops 8192 | bytes 65536 | tf_op jit(solution)/shard_map/psum | solution.py:63
  277.0 0.6 dynamic_slice.3
  277.6 0.0 all-to-all-done.2
  277.6 0.1 reshape.96
  277.7 1.4 gather_fusion.1
  (10 shorter events, 0.1 us)
Async XLA Ops:
  0.6 0.7 copy-start.3
  1.3 26.4 %copy-start.2 = (bf16[1024]{0:T(1024)(128)(2,1)S(1)}, bf16[1024]{0:T(1024)(128)(2,1)}, u32[]{:S(2)}) copy-start(bf16[1024]{0:T(1024)(128)(2,1)} %param.8) | copy-start | bytes 6148
  1.3 84.1 %copy-start = (bf16[128,8192]{1,0:T(8,128)(2,1)S(1)}, bf16[128,8192]{1,0:T(8,128)(2,1)}, u32[]{:S(2)}) copy-start(bf16[128,8192]{1,0:T(8,128)(2,1)} %param.5) | copy-start | bytes 6291460
  2.9 20.6 %all-to-all-start = ((s32[8,1,4]{2,1,0:T(1,128)}), s32[8,1,4]{2,1,0:T(1,128)S(1)}, u32[]{:S(2)}, u32[]{:S(2)}) async-start(s32[8,1,4]{2,1,0:T(1,128)} %bitcast), calls=%async_computation | async-start | bytes 8192 | tf_op jit(solution)/shard_map/all_to_all | solution.py:45
  23.6 38.8 %all-to-all-start.1 = ((bf16[8,4,8192]{2,1,0:T(4,128)(2,1)}), bf16[8,4,8192]{2,1,0:T(4,128)(2,1)S(1)}, u32[]{:S(2)}, u32[]{:S(2)}) async-start(bf16[8,4,8192]{2,1,0:T(4,128)(2,1)} %reshape.94), calls=%async_computation.1 | async-start | bytes 1048576 | tf_op jit(solution)/shard_map/all_to_all | solution.py:44
  48.5 13.7 %collective-permute-start = (s32[8,4]{0,1:T(4,128)S(1)}, s32[8,4]{0,1:T(4,128)S(1)}, u32[]{:S(2)}, u32[]{:S(2)}) collective-permute-start(s32[8,4]{0,1:T(4,128)S(1)} %bitcast.6), channel_id=1, source_target_pairs={{0,192},{8,200},{16,208},{24,216},{32,224},{40,232},{48,240},{56,2... | collective-permute-start | bytes 392 | tf_op jit(solution)/shard_map/ppermute | solution.py:10
  62.4 23.0 %collective-permute-start.1 = (bf16[8,4,8192]{2,1,0:T(4,128)(2,1)S(1)}, bf16[8,4,8192]{2,1,0:T(4,128)(2,1)S(1)}, u32[]{:S(2)}, u32[]{:S(2)}) collective-permute-start(bf16[8,4,8192]{2,1,0:T(4,128)(2,1)S(1)} %all-to-all-done.1), channel_id=1, source_target_pairs={{0,192},{8,200},{16,208},{24,216},{32,224},{40,232},{48,240},{56,2... | collective-permute-start | bytes 1572872 | tf_op jit(solution)/shard_map/ppermute | solution.py:10
  87.9 1.6 copy-start.1
  97.8 27.1 %collective-permute-start.2 = (bf16[8,4,8192]{2,1,0:T(4,128)(2,1)S(1)}, bf16[8,4,8192]{2,1,0:T(4,128)(2,1)}, u32[]{:S(2)}, u32[]{:S(2)}) collective-permute-start(bf16[8,4,8192]{2,1,0:T(4,128)(2,1)S(1)} %broadcast_select_fusion), channel_id=1, source_target_pairs={{0,576},{8,584},{16,592},{24,600},{32,608},{40,616},{48,624},{56,6... | collective-permute-start | bytes 1572872 | tf_op jit(solution)/shard_map/ppermute | solution.py:10
  124.9 152.7 %all-to-all-start.2 = ((bf16[8,4,8192]{2,1,0:T(4,128)(2,1)}), bf16[8,4,8192]{2,1,0:T(4,128)(2,1)S(1)}, u32[]{:S(2)}, u32[]{:S(2)}) async-start(bf16[8,4,8192]{2,1,0:T(4,128)(2,1)} %collective-permute-done.2), calls=%async_computation.2 | async-start | bytes 1048576 | tf_op jit(solution)/shard_map/all_to_all | solution.py:58
where the time goes:
time: 280 us; the launch traced here: 279 us
  blocking collectives  167 us (60%)
  starting transfers between devices  55.1 us (20%)
  waiting for transfers between devices  36.1 us (13%)
  local copies, waits for them, and re-layouts  14 us (5%)
  other arithmetic  5.68 us (2%)
    psum x1, blocking collectives, shards(): total = lax.psum(terms, ('grp', 'fsdp'))  147 us
    ppermute x3, starting transfers between devices, shifted(): return lax.ppermute(value, axis, pairs)  31.9 us
    ppermute x3, waiting for transfers between devices, shifted(): return lax.ppermute(value, axis, pairs)  31.7 us
    all_gather x1, blocking collectives, shards(): lax.all_gather(gain, 'fsdp', axis=0, tiled=True).astype(jnp.float32)  20.8 us
    all_to_all x1, starting transfers between devices, shards(): lax.all_to_all(places, 'fsdp', split_axis=0, concat_axis=0, tiled=True)  13.7 us
  transfers between devices with their start and end apart: 6, of which 4 were waited for; matrix products, arithmetic and copies ran while one was open for 1% of the time, Pallas kernels for 0%

commit v1 on v0

v1 whole, which is shorter than its diff:
```python
import jax
import jax.numpy as jnp
from jax import lax
from jax.sharding import Mesh, PartitionSpec as P

AXES = ("ylo", "zhi", "zlo", "x", "yhi", "core")
QUARTER = ("ylo", "zhi")
GRP = ("ylo", "zhi", "zlo", "x")
FSDP = ("yhi", "core")
PLANE = ("yhi", "core", "ylo", "x")
SIZES = (2, 2, 6, 4, 4, 2)
N_QUARTER = 4
N_FSDP = 8
CAP = 4


def exchange(value, axes):
    return lax.all_to_all(value, axes, split_axis=0, concat_axis=0, tiled=True)


def turned(value, steps):
    pairs = [(source, (source + steps) % N_QUARTER) for source in range(N_QUARTER)]
    return lax.ppermute(value, QUARTER, pairs)


def select_rows(onehot, rows):
    picked = lax.dot_general(
        onehot, rows, (((1,), (0,)), ((), ())), preferred_element_type=jnp.float32
    )
    return picked.astype(rows.dtype)


def shards(text, vision, vision_token, gain, cotangent):
    tok_dev, width = text.shape
    vis_dev = vision.shape[0]
    quarter = lax.axis_index(QUARTER)
    me = lax.axis_index(FSDP)

    tokens = exchange(
        jnp.broadcast_to(vision_token[None, :], (N_QUARTER * N_FSDP, vis_dev)), QUARTER + FSDP
    ).reshape(N_QUARTER, N_FSDP, vis_dev)
    from_quarter = (quarter + N_QUARTER - 1) % N_QUARTER
    tokens = jnp.sum(
        jnp.where(jnp.arange(N_QUARTER)[:, None, None] == from_quarter, tokens, 0), axis=0
    )
    rows = turned(vision, 1)
    full_gain = exchange(jnp.broadcast_to(gain[None, :], (N_FSDP, gain.shape[0])), FSDP)
    full_gain = full_gain.reshape(1, width).astype(jnp.float32)

    target = tokens // tok_dev % N_FSDP
    local = tokens % tok_dev
    same = target[:, :, None] == target[:, None, :]
    before = jnp.arange(vis_dev)[None, :] < jnp.arange(vis_dev)[:, None]
    rank = jnp.sum((same & before[None]).astype(jnp.int32), axis=2)

    sends = (target == me)[:, None, :] & (rank[:, None, :] == jnp.arange(CAP)[None, :, None])
    place = jnp.sum(jnp.where(sends, local[:, None, :] + 1, 0), axis=2).reshape(N_FSDP * CAP, 1) - 1
    pick = place == jnp.arange(tok_dev)[None, :]
    sent = select_rows(pick.astype(jnp.bfloat16), cotangent).reshape(N_FSDP, CAP, width)
    arrived = exchange(sent, FSDP).reshape(N_FSDP * CAP, width)

    values = text.astype(jnp.float32)
    upper = cotangent.astype(jnp.float32)
    inv = lax.rsqrt(jnp.mean(values * values, axis=-1, keepdims=True) + 1e-06)
    kept = jnp.where(jnp.any(pick, axis=0)[:, None], 0.0, inv)
    terms = jnp.sum(upper * values * kept, axis=0)

    mine = jnp.arange(N_FSDP)[:, None] == me
    slot = jnp.sum(jnp.where(mine, target * CAP + rank, 0), axis=0)[:, None]
    order = slot == jnp.arange(N_FSDP * CAP)[None, :]
    upper_v = select_rows(order.astype(jnp.bfloat16), arrived).astype(jnp.float32)
    values_v = rows.astype(jnp.float32)
    inv_v = lax.rsqrt(jnp.mean(values_v * values_v, axis=-1, keepdims=True) + 1e-06)
    scaled = upper_v * full_gain
    inner = jnp.mean(values_v * scaled, axis=-1, keepdims=True)
    grad = inv_v * scaled - values_v * inv_v * inv_v * inv_v * inner
    vision_grad = turned(grad.astype(jnp.bfloat16), -1)
    terms = terms + jnp.sum(upper_v * values_v * inv_v, axis=0)

    lanes = width // 64
    part = jnp.sum(exchange(terms.reshape(64, lanes), PLANE), axis=0)
    parts = exchange(jnp.broadcast_to(part[None, :], (96, lanes)), GRP)
    gain_grad = jnp.sum(parts.reshape(2, 12, 4, lanes), axis=1).reshape(width // N_FSDP)
    return (vision_grad, gain_grad)


def solution(mesh):
    fine = Mesh(mesh.devices.reshape(SIZES), AXES)
    return jax.shard_map(
        shards,
        mesh=fine,
        in_specs=(P(AXES, None), P(AXES, None), P(AXES), P(FSDP), P(AXES, None)),
        out_specs=(P(AXES, None), P(FSDP)),
        check_vma=False,
    )
```

time: 280 us -> 120 us (0.43)
  blocking collectives: 167 us -> 41.1 us
  waiting for transfers between devices: 36.1 us -> 19.5 us
  starting transfers between devices: 55.1 us -> 44.9 us
  local copies, waits for them, and re-layouts: 14 us -> 5.13 us
    psum x1 -> x0, blocking collectives: 147 us -> none  [shards(): total = lax.psum(terms, ('grp', 'fsdp'))]
    all_to_all x0 -> x2, blocking collectives: none -> 41.1 us  [exchange(): return lax.all_to_all(value, axes, split_axis=0, concat_axis=0, tiled=True)]
    ppermute x3 -> x2, waiting for transfers between devices: 31.7 us -> 0.01 us  [turned(): return lax.ppermute(value, QUARTER, pairs)]
    all_gather x1 -> x0, blocking collectives: 20.8 us -> none  [shards(): lax.all_gather(gain, 'fsdp', axis=0, tiled=True).astype(jnp.float32)]
    ppermute x3 -> x2, starting transfers between devices: 31.9 us -> 14.1 us  [turned(): return lax.ppermute(value, QUARTER, pairs)]
    all_to_all x3, waiting for transfers between devices: 4.43 us -> 19.5 us  [exchange(): return lax.all_to_all(value, axes, split_axis=0, concat_axis=0, tiled=True)]
    all_to_all x3, starting transfers between devices: 23.2 us -> 30.9 us  [exchange(): return lax.all_to_all(value, axes, split_axis=0, concat_axis=0, tiled=True)]
    gather x3 -> x0, local copies, waits for them, and re-layouts: 4.82 us -> none  [the longest x2 3.4 us: shards(): jnp.take(token_grad, jnp.minimum(arrived_places, tok_dev - 1), axis=0)]
  transfers between devices with their start and end apart: 6 -> 5, of which waited for: 4 -> 3; matrix products, arithmetic and copies ran while one was open for 1% -> 9% of each run, Pallas kernels for 0% -> 0%
where the time goes in v1:
time: 120 us
  starting transfers between devices  44.9 us (37%)
  blocking collectives  41.1 us (34%)
  waiting for transfers between devices  19.5 us (16%)
  other arithmetic  5.4 us (4%)
  local copies, waits for them, and re-layouts  5.13 us (4%)
  matrix products  2.69 us (2%)
    all_to_all x2, blocking collectives, exchange(): return lax.all_to_all(value, axes, split_axis=0, concat_axis=0, tiled=True)  41.1 us
    all_to_all x3, starting transfers between devices, exchange(): return lax.all_to_all(value, axes, split_axis=0, concat_axis=0, tiled=True)  30.9 us
    all_to_all x3, waiting for transfers between devices, exchange(): return lax.all_to_all(value, axes, split_axis=0, concat_axis=0, tiled=True)  19.5 us
    ppermute x2, starting transfers between devices, turned(): return lax.ppermute(value, QUARTER, pairs)  14.1 us
    dot_general x2, matrix products, select_rows(): lax.dot_general(onehot, rows, (((1,), (0,)), ((), ())), preferred_element...  2.69 us
  transfers between devices with their start and end apart: 5, of which 3 were waited for; matrix products, arithmetic and copies ran while one was open for 9% of the time, Pallas kernels for 0%

profile of v1, /device:TPU:1, one launch (start us, length us, event | category | flops | bytes accessed | tf_op | source)
XLA Modules:
  0.0 119.5 jit_solution(598394876499186360)
XLA Ops:
  0.6 1.3 %broadcast_in_dim.42 = s32[32,1,16]{2,1,0:T(1,128)} broadcast(s32[16]{0:T(128)} %param.7), dimensions={2} | broadcast | bytes 2112 | tf_op jit(solution)/shard_map/broadcast_in_dim | solution.py:40
  1.9 21.4 %all-to-all-start = ((s32[32,1,16]{2,1,0:T(1,128)}), s32[32,1,16]{2,1,0:T(1,128)S(1)}, u32[]{:S(2)}, u32[]{:S(2)}) async-start(s32[32,1,16]{2,1,0:T(1,128)} %broadcast_in_dim.42), calls=%async_computation | async-start | bytes 32768 | tf_op jit(solution)/shard_map/all_to_all | solution.py:18
  23.3 9.6 %collective-permute-start = (bf16[16,8192]{1,0:T(8,128)(2,1)}, bf16[16,8192]{1,0:T(8,128)(2,1)S(1)}, u32[]{:S(2)}, u32[]{:S(2)}) collective-permute-start(bf16[16,8192]{1,0:T(8,128)(2,1)} %param.6), channel_id=1, source_target_pairs={{0,192},{192,384},{384,576},{576,0},{1,193},{193,385},{385,577},{5... | collective-permute-start | bytes 786440 | tf_op jit(solution)/shard_map/ppermute | solution.py:23
  33.0 0.7 broadcast_in_dim.50
  33.7 0.5 broadcast.269
  34.2 0.7 reduce.1
  34.9 0.6 reshape.214
  35.5 2.0 %all-to-all-done = s32[32,1,16]{2,1,0:T(1,128)S(1)} async-done(((s32[32,1,16]{2,1,0:T(1,128)}), s32[32,1,16]{2,1,0:T(1,128)S(1)}, u32[]{:S(2)}, u32[]{:S(2)}) %all-to-all-start) | async-done | bytes 2080 | tf_op jit(solution)/shard_map/all_to_all | solution.py:18
  37.5 5.4 %all-to-all-start.2 = ((bf16[8,2,512]{2,1,0:T(2,128)(2,1)}), bf16[8,2,512]{2,1,0:T(2,128)(2,1)S(1)}, u32[]{:S(2)}, u32[]{:S(2)}) async-start(bf16[8,2,512]{2,1,0:T(2,128)(2,1)} %reshape.214), calls=%async_computation.2 | async-start | bytes 32768 | tf_op jit(solution)/shard_map/all_to_all | solution.py:18
  42.9 0.1 fusion.13
  43.0 0.3 convert_reduce_fusion
  43.2 0.2 select_reduce_fusion
  43.4 0.1 copy.8
  43.5 0.1 sub.21
  43.6 0.0 copy-start.1
  43.6 2.2 %convolution_convert_fusion = bf16[32,8192]{1,0:T(8,128)(2,1)S(1)} fusion(bf16[128,8192]{1,0:T(8,128)(2,1)} %param.9, s32[32]{0:T(128)S(1)} %sub.21), kind=kOutput, calls=%fused_computation | convolution fusion | flops 67375104 | bytes 2621568 | tf_op jit(solution)/shard_map/dot_general | solution.py:27
  45.8 1.0 reshape.209
  46.8 3.1 %all-to-all-done.2 = bf16[8,2,512]{2,1,0:T(2,128)(2,1)S(1)} async-done(((bf16[8,2,512]{2,1,0:T(2,128)(2,1)}), bf16[8,2,512]{2,1,0:T(2,128)(2,1)S(1)}, u32[]{:S(2)}, u32[]{:S(2)}) %all-to-all-start.2) | async-done | bytes 16416 | tf_op jit(solution)/shard_map/all_to_all | solution.py:18
  49.9 4.1 %all-to-all-start.1 = ((bf16[8,4,8192]{2,1,0:T(4,128)(2,1)}), bf16[8,4,8192]{2,1,0:T(4,128)(2,1)S(1)}, u32[]{:S(2)}, u32[]{:S(2)}) async-start(bf16[8,4,8192]{2,1,0:T(4,128)(2,1)} %reshape.209), calls=%async_computation.1 | async-start | bytes 1048576 | tf_op jit(solution)/shard_map/all_to_all | solution.py:18
  54.0 0.0 copy-done.1
  54.0 0.5 fusion.3
  54.5 0.0 copy-start
  54.5 0.1 select_reduce_fusion.1
  54.6 0.1 fusion.14
  54.8 0.0 collective-permute-done
  54.8 0.2 fusion.4
  55.0 14.4 %all-to-all-done.1 = bf16[8,4,8192]{2,1,0:T(4,128)(2,1)S(1)} async-done(((bf16[8,4,8192]{2,1,0:T(4,128)(2,1)}), bf16[8,4,8192]{2,1,0:T(4,128)(2,1)S(1)}, u32[]{:S(2)}, u32[]{:S(2)}) %all-to-all-start.1) | async-done | bytes 524320 | tf_op jit(solution)/shard_map/all_to_all | solution.py:18
  69.4 0.1 reshape.210
  69.5 0.5 fusion.12
  70.0 0.2 fusion.9
  70.2 4.5 %collective-permute-start.1 = (bf16[16,8192]{1,0:T(8,128)(2,1)S(1)}, bf16[16,8192]{1,0:T(8,128)(2,1)S(1)}, u32[]{:S(2)}, u32[]{:S(2)}) collective-permute-start(bf16[16,8192]{1,0:T(8,128)(2,1)S(1)} %fusion.9), channel_id=1, source_target_pairs={{0,576},{192,0},{384,192},{576,384},{1,577},{193,1},{385,193},{577... | collective-permute-start | bytes 786440 | tf_op jit(solution)/shard_map/ppermute | solution.py:23
  74.7 0.0 copy-done
  74.7 2.3 %fusion.2 = f32[8192]{0:T(1024)S(1)} fusion(bf16[128,8192]{1,0:T(8,128)(2,1)} %param.5, bf16[128,8192]{1,0:T(8,128)(2,1)S(1)} %copy-done, f32[128]{0:T(128)S(1)} %rsqrt_select_fusion), kind=kLoop, calls=%fused_computation.6 | loop fusion | flops 5234688 | bytes 4227584 | tf_op jit(solution)/shard_map/reduce_sum | solution.py:66
  77.1 15.9 %all_to_all.29 = f32[64,1,128]{2,1,0:T(1,128)S(1)} all-to-all(f32[64,1,128]{2,1,0:T(1,128)S(1)} %bitcast.15), channel_id=1, replica_groups=mesh['ylo'=2,'zhi'=2,'zlo'=6,'x'=4,'yhi'=4,'core'=2] {'yhi','core','ylo'..., dimensions={0} | all-to-all | bytes 65536 | tf_op jit(solution)/shard_map/all_to_all | solution.py:18
  93.0 25.2 %all_to_all.30 = f32[96,1,128]{2,1,0:T(1,128)S(1)} all-to-all(f32[96,1,128]{2,1,0:T(1,128)S(1)} %broadcast_in_dim.52), channel_id=1, replica_groups=mesh['ylo'=2,'zhi'=2,'zlo'=6,'x'=4,'yhi'=4,'core'=2] {'ylo','zhi','zlo',..., dimensions={0} | all-to-all | bytes 98304 | tf_op jit(solution)/shard_map/all_to_all | solution.py:18
  118.2 0.6 reduce_sum.109
  118.8 0.0 collective-permute-done.1
  118.8 0.7 copy.11
  (14 shorter events, 0.2 us)
Async XLA Ops:
  1.9 35.6 %all-to-all-start = ((s32[32,1,16]{2,1,0:T(1,128)}), s32[32,1,16]{2,1,0:T(1,128)S(1)}, u32[]{:S(2)}, u32[]{:S(2)}) async-start(s32[32,1,16]{2,1,0:T(1,128)} %broadcast_in_dim.42), calls=%async_computation | async-start | bytes 32768 | tf_op jit(solution)/shard_map/all_to_all | solution.py:18
  23.3 31.5 %collective-permute-start = (bf16[16,8192]{1,0:T(8,128)(2,1)}, bf16[16,8192]{1,0:T(8,128)(2,1)S(1)}, u32[]{:S(2)}, u32[]{:S(2)}) collective-permute-start(bf16[16,8192]{1,0:T(8,128)(2,1)} %param.6), channel_id=1, source_target_pairs={{0,192},{192,384},{384,576},{576,0},{1,193},{193,385},{385,577},{5... | collective-permute-start | bytes 786440 | tf_op jit(solution)/shard_map/ppermute | solution.py:23
  37.5 12.4 %all-to-all-start.2 = ((bf16[8,2,512]{2,1,0:T(2,128)(2,1)}), bf16[8,2,512]{2,1,0:T(2,128)(2,1)S(1)}, u32[]{:S(2)}, u32[]{:S(2)}) async-start(bf16[8,2,512]{2,1,0:T(2,128)(2,1)} %reshape.214), calls=%async_computation.2 | async-start | bytes 32768 | tf_op jit(solution)/shard_map/all_to_all | solution.py:18
  43.6 10.5 %copy-start.1 = (bf16[128,8192]{1,0:T(8,128)(2,1)S(1)}, bf16[128,8192]{1,0:T(8,128)(2,1)}, u32[]{:S(2)}) copy-start(bf16[128,8192]{1,0:T(8,128)(2,1)} %param.5) | copy-start | bytes 6291460
  49.9 19.4 %all-to-all-start.1 = ((bf16[8,4,8192]{2,1,0:T(4,128)(2,1)}), bf16[8,4,8192]{2,1,0:T(4,128)(2,1)S(1)}, u32[]{:S(2)}, u32[]{:S(2)}) async-start(bf16[8,4,8192]{2,1,0:T(4,128)(2,1)} %reshape.209), calls=%async_computation.1 | async-start | bytes 1048576 | tf_op jit(solution)/shard_map/all_to_all | solution.py:18
  54.5 20.2 %copy-start = (bf16[128,8192]{1,0:T(8,128)(2,1)S(1)}, bf16[128,8192]{1,0:T(8,128)(2,1)}, u32[]{:S(2)}) copy-start(bf16[128,8192]{1,0:T(8,128)(2,1)} %param.9) | copy-start | bytes 6291460
  70.2 48.6 %collective-permute-start.1 = (bf16[16,8192]{1,0:T(8,128)(2,1)S(1)}, bf16[16,8192]{1,0:T(8,128)(2,1)S(1)}, u32[]{:S(2)}, u32[]{:S(2)}) collective-permute-start(bf16[16,8192]{1,0:T(8,128)(2,1)S(1)} %fusion.9), channel_id=1, source_target_pairs={{0,576},{192,0},{384,192},{576,384},{1,577},{193,1},{385,193},{577... | collective-permute-start | bytes 786440 | tf_op jit(solution)/shard_map/ppermute | solution.py:23

commit v2 on v1

v2 whole, which is shorter than its diff:
```python
import jax
import jax.numpy as jnp
from jax import lax
from jax.experimental import pallas as pl
from jax.experimental.pallas import tpu as pltpu
from jax.sharding import Mesh, PartitionSpec as P

AXES = ("ylo", "zhi", "zlo", "x", "yhi", "core")
QUARTER = ("ylo", "zhi")
GRP = ("ylo", "zhi", "zlo", "x")
FSDP = ("yhi", "core")
PLANE = ("yhi", "core", "ylo", "x")
SIZES = (2, 2, 6, 4, 4, 2)
DEVICES = 768
N_QUARTER = 4
N_FSDP = 8
CAP = 4
TOK = 128
VIS = 16
WIDTH = 8192
HALF = WIDTH // 2
LANES = 128
SLOTS = N_FSDP * 2 * CAP
BLOCKS = WIDTH // LANES
F32 = jnp.float32
BF16 = jnp.bfloat16
VMEM = pl.BlockSpec(memory_space=pltpu.VMEM)
SMEM = pl.BlockSpec(memory_space=pltpu.SMEM)


def iota(shape, dim):
    return lax.broadcasted_iota(jnp.int32, shape, dim)


def dot(a, b):
    return jnp.dot(a, b, preferred_element_type=F32)


def pack_kernel(dev_ref, tok_ref, gain_ref, cot_ref, sent_ref, order_ref, taken_ref):
    dev = dev_ref[0]
    source = lax.rem(dev // (DEVICES // N_QUARTER) + N_QUARTER - 1, N_QUARTER) * N_FSDP
    tokens = tok_ref[pl.ds(pl.multiple_of(source, N_FSDP), N_FSDP), :]
    position = dev * TOK + iota((N_FSDP, TOK), 1)
    count = jnp.zeros((N_FSDP, TOK), jnp.int32)
    chosen = [jnp.zeros((N_FSDP, TOK), F32)] * CAP
    for i in range(VIS):
        token = jnp.broadcast_to(tokens[:, i : i + 1], (N_FSDP, TOK))
        hit = token == position
        for r in range(CAP):
            chosen[r] = jnp.where(hit & (count == r), 1.0, chosen[r])
        count = count + jnp.where((token >> 7) == dev, 1, 0)
    chosen = jnp.concatenate(chosen, axis=0)
    taken_ref[...] = jnp.broadcast_to(jnp.sum(chosen, axis=0, keepdims=True), taken_ref.shape)
    chosen = chosen.astype(BF16)
    row, col = iota((SLOTS, N_FSDP * CAP), 0), iota((SLOTS, N_FSDP * CAP), 1)
    halves = []
    for half in range(2):
        at = ((col & 7) == (row >> 3)) & ((col >> 3) + CAP * half == (row & 7))
        halves.append(dot(jnp.where(at, 1.0, 0.0).astype(BF16), chosen).astype(BF16))
    lhs = jnp.concatenate(halves, axis=1)
    step = 512
    for k in range(0, HALF, step):
        rhs = jnp.concatenate([cot_ref[:, k : k + step], cot_ref[:, HALF + k : HALF + k + step]], axis=0)
        sent_ref[:, k : k + step] = dot(lhs, rhs).astype(BF16)
    gain = gain_ref[...].astype(F32)
    sent_ref[:, HALF:] = jnp.concatenate([gain] * N_FSDP, axis=0).astype(BF16)
    own = jnp.broadcast_to(tok_ref[pl.ds(source + lax.rem(dev, N_FSDP), 1), :], (VIS, VIS))
    i, j = iota((VIS, VIS), 0), iota((VIS, VIS), 1)
    target = ((own >> 7) & (N_FSDP - 1)).astype(F32)
    mine = jnp.sum(jnp.where(i == j, target, 0.0), axis=1, keepdims=True)
    rank = jnp.sum(jnp.where((target == mine) & (j < i), 1.0, 0.0), axis=1, keepdims=True)
    slot = (mine * 8.0 + rank).astype(jnp.int32)
    at = iota((VIS, SLOTS), 1)
    order = [jnp.where(at == slot + CAP * half, 1.0, 0.0) for half in range(2)]
    order_ref[...] = jnp.concatenate(order, axis=0).astype(BF16)


def terms_kernel(order_ref, arrived_ref, unit_ref, text_ref, terms_ref, upper_ref):
    step = 8 * LANES
    for k in range(0, WIDTH, step):
        half, at = divmod(k, HALF)
        upper = dot(order_ref[half * VIS : (half + 1) * VIS, :], arrived_ref[:, at : at + step])
        upper_ref[:, k : k + step] = upper.astype(BF16)
        product = upper * unit_ref[:, k : k + step]
        total = jnp.sum(product, axis=0, keepdims=True)
        block = k // LANES
        rows = [total[:, b * LANES : (b + 1) * LANES] for b in range(8)]
        terms_ref[block : block + 8, :] = text_ref[block : block + 8, :] + jnp.concatenate(rows, axis=0)


def grads_kernel(arrived_ref, upper_ref, unit_ref, inv_ref, grad_ref):
    total = jnp.zeros((VIS, LANES), F32)
    for b in range(BLOCKS):
        at = slice(b * LANES, (b + 1) * LANES)
        gain = arrived_ref[b : b + 1, HALF:].astype(F32)
        total = total + upper_ref[:, at].astype(F32) * gain * unit_ref[:, at]
    inner = jnp.sum(total, axis=1, keepdims=True) * (1.0 / WIDTH)
    inv = inv_ref[...]
    for b in range(BLOCKS):
        at = slice(b * LANES, (b + 1) * LANES)
        gain = arrived_ref[b : b + 1, HALF:].astype(F32)
        scaled = upper_ref[:, at].astype(F32) * gain
        grad_ref[:, at] = (inv * (scaled - unit_ref[:, at] * inner)).astype(BF16)


def kernel_call(body, outs, in_specs, cost):
    return pl.pallas_call(
        body,
        out_shape=outs,
        in_specs=in_specs,
        out_specs=[VMEM] * len(outs),
        compiler_params=pltpu.CompilerParams(vmem_limit_bytes=16 * 2**20),
        cost_estimate=pl.CostEstimate(flops=cost, bytes_accessed=cost, transcendentals=0),
    )


def exchange(value, axes):
    return lax.all_to_all(value, axes, split_axis=0, concat_axis=0, tiled=True)


def turned(value, steps):
    pairs = [(source, (source + steps) % N_QUARTER) for source in range(N_QUARTER)]
    return lax.ppermute(value, QUARTER, pairs)


def shape(*dims, dtype=F32):
    return jax.ShapeDtypeStruct(dims, dtype)


def program(text, vision, vision_token, gain, cotangent):
    device = jnp.full((1,), lax.axis_index(AXES), jnp.int32)
    tokens = exchange(
        jnp.broadcast_to(vision_token[None, :], (N_QUARTER * N_FSDP, VIS)), QUARTER + FSDP
    )
    rows = turned(vision, 1)

    sent, order, taken = kernel_call(
        pack_kernel,
        [shape(SLOTS, HALF + LANES, dtype=BF16), shape(2 * VIS, SLOTS, dtype=BF16), shape(8, TOK)],
        [SMEM, VMEM, VMEM, VMEM],
        2 * 2**20,
    )(device, tokens, gain.reshape(8, LANES), cotangent)
    arrived = exchange(sent, FSDP)

    values = text.astype(F32)
    inv = lax.rsqrt(jnp.mean(values * values, axis=-1, keepdims=True) + 1e-06)
    kept = jnp.where(taken[0][:, None] > 0.0, 0.0, inv)
    text_terms = jnp.sum(cotangent.astype(F32) * values * kept, axis=0)

    values_v = rows.astype(F32)
    inv_v = lax.rsqrt(jnp.mean(values_v * values_v, axis=-1, keepdims=True) + 1e-06)
    unit = values_v * inv_v
    terms, upper = kernel_call(
        terms_kernel, [shape(BLOCKS, LANES), shape(VIS, WIDTH, dtype=BF16)], [VMEM] * 4, 2**20
    )(order, arrived, unit, text_terms.reshape(BLOCKS, LANES))
    (grad,) = kernel_call(grads_kernel, [shape(VIS, WIDTH, dtype=BF16)], [VMEM] * 4, 2**20)(
        arrived, upper, unit, jnp.broadcast_to(inv_v, (VIS, LANES))
    )
    vision_grad = turned(grad, -1)

    pieces = exchange(terms, PLANE)
    part = jnp.sum(pieces, axis=0)
    parts = exchange(jnp.broadcast_to(part[None, :], (DEVICES // N_FSDP, LANES)), GRP)
    gain_grad = jnp.sum(parts.reshape(2, 12, 4, LANES), axis=1).reshape(WIDTH // N_FSDP)
    return (vision_grad, gain_grad)


def solution(mesh):
    fine = Mesh(mesh.devices.reshape(SIZES), AXES)
    return jax.shard_map(
        program,
        mesh=fine,
        in_specs=(P(AXES, None), P(AXES, None), P(AXES), P(FSDP), P(AXES, None)),
        out_specs=(P(AXES, None), P(FSDP)),
        check_vma=False,
    )
```

time: 120 us -> 111 us (0.925)
  starting transfers between devices: 44.9 us -> 40.2 us
  waiting for transfers between devices: 19.5 us -> 15.3 us
  blocking collectives: 41.1 us -> 44.3 us
  local copies, waits for them, and re-layouts: 5.13 us -> 2.23 us
  matrix products: 2.69 us -> 0 us
  Pallas kernels: 0 us -> 2 us
    all_to_all x3 -> x2, starting transfers between devices: 30.9 us -> 26.3 us  [exchange(): return lax.all_to_all(value, axes, split_axis=0, concat_axis=0, tiled=True)]
    all_to_all x3 -> x2, waiting for transfers between devices: 19.5 us -> 15.3 us  [exchange(): return lax.all_to_all(value, axes, split_axis=0, concat_axis=0, tiled=True)]
    all_to_all x2, blocking collectives: 41.1 us -> 44.3 us  [exchange(): return lax.all_to_all(value, axes, split_axis=0, concat_axis=0, tiled=True)]
    dot_general x2 -> x0, matrix products: 2.69 us -> none  [select_rows(): lax.dot_general(onehot, rows, (((1,), (0,)), ((), ())), preferred_element...]
    pallas_call x0 -> x3, Pallas kernels: none -> 2 us  [the longest x1 1.48 us: program(): kernel_call(pack_kernel, [shape(SLOTS, HALF + LANES, dtype=BF16), shape(2...]
    reduce_sum x9 -> x5, other arithmetic: 4.25 us -> 5.31 us  [the longest x1 2.34 us: program(): text_terms = jnp.sum(cotangent.astype(F32) * values * kept, axis=0)]
    broadcast_in_dim x4 -> x3, local copies, waits for them, and re-layouts: 2.51 us -> 1.52 us  [the longest x1 1.42 us: program(): jnp.broadcast_to(vision_token[None, :], (N_QUARTER * N_FSDP, VIS))]
  transfers between devices with their start and end apart: 5 -> 4, of which waited for: 3 -> 2; matrix products, arithmetic and copies ran while one was open for 9% -> 5% of each run, Pallas kernels for 0% -> 1%
where the time goes in v2:
time: 111 us; the launch traced here: 110 us
  blocking collectives  44.3 us (40%)
  starting transfers between devices  40.2 us (36%)
  waiting for transfers between devices  15.3 us (14%)
  other arithmetic  5.43 us (5%)
  local copies, waits for them, and re-layouts  2.23 us (2%)
  Pallas kernels  2 us (2%)
    all_to_all x2, blocking collectives, exchange(): return lax.all_to_all(value, axes, split_axis=0, concat_axis=0, tiled=True)  44.3 us
    all_to_all x2, starting transfers between devices, exchange(): return lax.all_to_all(value, axes, split_axis=0, concat_axis=0, tiled=True)  26.3 us
    all_to_all x2, waiting for transfers between devices, exchange(): return lax.all_to_all(value, axes, split_axis=0, concat_axis=0, tiled=True)  15.3 us
    ppermute x2, starting transfers between devices, turned(): return lax.ppermute(value, QUARTER, pairs)  13.9 us
    reduce_sum x1, other arithmetic, program(): text_terms = jnp.sum(cotangent.astype(F32) * values * kept, axis=0)  2.34 us
  transfers between devices with their start and end apart: 4, of which 2 were waited for; matrix products, arithmetic and copies ran while one was open for 5% of the time, Pallas kernels for 1%

profile of v2, /device:TPU:1, one launch (start us, length us, event | category | flops | bytes accessed | tf_op | source)
XLA Modules:
  0.0 110.3 jit_solution(11022037243207730049)
XLA Ops:
  0.6 0.0 copy-start.1
  0.6 0.0 copy-start
  0.7 1.4 %broadcast_in_dim.11 = s32[32,1,16]{2,1,0:T(1,128)} broadcast(s32[16]{0:T(128)} %param.7), dimensions={2} | broadcast | bytes 2112 | tf_op jit(solution)/shard_map/broadcast_in_dim | solution.py:133
  2.1 21.4 %all-to-all-start = ((s32[32,1,16]{2,1,0:T(1,128)}), s32[32,1,16]{2,1,0:T(1,128)S(1)}, u32[]{:S(2)}, u32[]{:S(2)}) async-start(s32[32,1,16]{2,1,0:T(1,128)} %broadcast_in_dim.11), calls=%async_computation | async-start | bytes 32768 | tf_op jit(solution)/shard_map/all_to_all | solution.py:118
  23.5 9.6 %collective-permute-start = (bf16[16,8192]{1,0:T(8,128)(2,1)}, bf16[16,8192]{1,0:T(8,128)(2,1)S(1)}, u32[]{:S(2)}, u32[]{:S(2)}) collective-permute-start(bf16[16,8192]{1,0:T(8,128)(2,1)} %param.6), channel_id=1, source_target_pairs={{0,192},{192,384},{384,576},{576,0},{1,193},{193,385},{385,577},{5... | collective-permute-start | bytes 786440 | tf_op jit(solution)/shard_map/ppermute | solution.py:123
  33.1 2.1 %fusion.2 = f32[128]{0:T(128)S(1)} fusion(bf16[128,8192]{1,0:T(8,128)(2,1)} %param.5), kind=kLoop, calls=%fused_computation.4 | loop fusion | flops 3145600 | bytes 2097664 | tf_op jit(solution)/shard_map/reduce_sum | solution.py:146
  35.2 2.4 %all-to-all-done = s32[32,1,16]{2,1,0:T(1,128)S(1)} async-done(((s32[32,1,16]{2,1,0:T(1,128)}), s32[32,1,16]{2,1,0:T(1,128)S(1)}, u32[]{:S(2)}, u32[]{:S(2)}) %all-to-all-start) | async-done | bytes 2080 | tf_op jit(solution)/shard_map/all_to_all | solution.py:118
  37.6 0.0 copy-done.1
  37.6 0.0 copy-done
  37.6 1.5 %shard_map.68 = (bf16[64,4224]{1,0:T(8,128)(2,1)}, bf16[32,64]{1,0:T(8,128)(2,1)S(1)}, f32[8,128]{1,0:T(8,128)S(1)}) custom-call(s32[1]{0:T(128)} %bitcast.dev_ref, s32[32,16]{1,0:T(8,128)S(1)} %bitcast.16, bf16[8,128]{1,0:T(8,128)(2,1)S(1)} %bitcast.18, bf16[128,8192]{1,0:T(8,128)(2,1)S(1)} %copy-done), custom_call_target="tpu_custom_call" | custom-call | flops 2097152 | bytes 2097152 | tf_op jit(solution)/shard_map/pallas_call | solution.py:137
  39.1 4.9 %all-to-all-start.1 = ((bf16[8,8,4224]{2,1,0:T(8,128)(2,1)}), bf16[8,8,4224]{2,1,0:T(8,128)(2,1)S(1)}, u32[]{:S(2)}, u32[]{:S(2)}) async-start(bf16[8,8,4224]{2,1,0:T(8,128)(2,1)} %bitcast.3), calls=%async_computation.1 | async-start | bytes 1081344 | tf_op jit(solution)/shard_map/all_to_all | solution.py:118
  44.0 2.3 %fusion.1 = f32[8192]{0:T(1024)S(1)} fusion(bf16[128,8192]{1,0:T(8,128)(2,1)} %param.5, bf16[128,8192]{1,0:T(8,128)(2,1)S(1)} %copy-done, f32[128]{0:T(128)S(1)} %bitcast_select_fusion), kind=kLoop, calls=%fused_computation.3 | loop fusion | flops 5234688 | bytes 4227584 | tf_op jit(solution)/shard_map/reduce_sum | solution.py:148
  46.4 0.0 collective-permute-done
  46.4 0.2 fusion.3
  46.6 0.1 convert_multiply_fusion.2.unit_ref
  46.7 12.9 %all-to-all-done.1 = bf16[8,8,4224]{2,1,0:T(8,128)(2,1)S(1)} async-done(((bf16[8,8,4224]{2,1,0:T(8,128)(2,1)}), bf16[8,8,4224]{2,1,0:T(8,128)(2,1)S(1)}, u32[]{:S(2)}, u32[]{:S(2)}) %all-to-all-start.1) | async-done | bytes 540704 | tf_op jit(solution)/shard_map/all_to_all | solution.py:118
  59.6 0.3 shard_map.69
  59.9 0.1 broadcast_in_dim.12.inv_ref
  59.9 0.3 shard_map.70
  60.2 4.3 %collective-permute-start.1 = (bf16[16,8192]{1,0:T(8,128)(2,1)S(1)}, bf16[16,8192]{1,0:T(8,128)(2,1)S(1)}, u32[]{:S(2)}, u32[]{:S(2)}) collective-permute-start(bf16[16,8192]{1,0:T(8,128)(2,1)S(1)} %shard_map.70), channel_id=1, source_target_pairs={{0,576},{192,0},{384,192},{576,384},{1,577},{193,1},{385,193},{577... | collective-permute-start | bytes 786440 | tf_op jit(solution)/shard_map/ppermute | solution.py:123
  64.5 16.1 %all_to_all.34 = f32[64,1,128]{2,1,0:T(1,128)S(1)} all-to-all(f32[64,1,128]{2,1,0:T(1,128)S(1)} %bitcast.17), channel_id=1, replica_groups=mesh['ylo'=2,'zhi'=2,'zlo'=6,'x'=4,'yhi'=4,'core'=2] {'yhi','core','ylo'..., dimensions={0} | all-to-all | bytes 65536 | tf_op jit(solution)/shard_map/all_to_all | solution.py:118
  80.6 0.1 reduce_sum.48
  80.7 28.2 %all_to_all.35 = f32[96,1,128]{2,1,0:T(1,128)S(1)} all-to-all(f32[96,1,128]{2,1,0:T(1,128)S(1)} %broadcast_in_dim.13), channel_id=1, replica_groups=mesh['ylo'=2,'zhi'=2,'zlo'=6,'x'=4,'yhi'=4,'core'=2] {'ylo','zhi','zlo',..., dimensions={0} | all-to-all | bytes 98304 | tf_op jit(solution)/shard_map/all_to_all | solution.py:118
  109.0 0.6 reduce_sum.49
  109.6 0.0 collective-permute-done.1
  109.6 0.7 copy.11
  (3 shorter events, 0.0 us)
Async XLA Ops:
  0.6 37.0 %copy-start.1 = (bf16[1024]{0:T(1024)(128)(2,1)S(1)}, bf16[1024]{0:T(1024)(128)(2,1)}, u32[]{:S(2)}) copy-start(bf16[1024]{0:T(1024)(128)(2,1)} %param.8) | copy-start | bytes 6148
  0.6 37.0 %copy-start = (bf16[128,8192]{1,0:T(8,128)(2,1)S(1)}, bf16[128,8192]{1,0:T(8,128)(2,1)}, u32[]{:S(2)}) copy-start(bf16[128,8192]{1,0:T(8,128)(2,1)} %cot_ref.1) | copy-start | bytes 6291460
  2.1 35.5 %all-to-all-start = ((s32[32,1,16]{2,1,0:T(1,128)}), s32[32,1,16]{2,1,0:T(1,128)S(1)}, u32[]{:S(2)}, u32[]{:S(2)}) async-start(s32[32,1,16]{2,1,0:T(1,128)} %broadcast_in_dim.11), calls=%async_computation | async-start | bytes 32768 | tf_op jit(solution)/shard_map/all_to_all | solution.py:118
  23.5 22.9 %collective-permute-start = (bf16[16,8192]{1,0:T(8,128)(2,1)}, bf16[16,8192]{1,0:T(8,128)(2,1)S(1)}, u32[]{:S(2)}, u32[]{:S(2)}) collective-permute-start(bf16[16,8192]{1,0:T(8,128)(2,1)} %param.6), channel_id=1, source_target_pairs={{0,192},{192,384},{384,576},{576,0},{1,193},{193,385},{385,577},{5... | collective-permute-start | bytes 786440 | tf_op jit(solution)/shard_map/ppermute | solution.py:123
  39.1 20.5 %all-to-all-start.1 = ((bf16[8,8,4224]{2,1,0:T(8,128)(2,1)}), bf16[8,8,4224]{2,1,0:T(8,128)(2,1)S(1)}, u32[]{:S(2)}, u32[]{:S(2)}) async-start(bf16[8,8,4224]{2,1,0:T(8,128)(2,1)} %bitcast.3), calls=%async_computation.1 | async-start | bytes 1081344 | tf_op jit(solution)/shard_map/all_to_all | solution.py:118
  60.2 49.4 %collective-permute-start.1 = (bf16[16,8192]{1,0:T(8,128)(2,1)S(1)}, bf16[16,8192]{1,0:T(8,128)(2,1)S(1)}, u32[]{:S(2)}, u32[]{:S(2)}) collective-permute-start(bf16[16,8192]{1,0:T(8,128)(2,1)S(1)} %shard_map.70), channel_id=1, source_target_pairs={{0,576},{192,0},{384,192},{576,384},{1,577},{193,1},{385,193},{577... | collective-permute-start | bytes 786440 | tf_op jit(solution)/shard_map/ppermute | solution.py:123

commit v3 on v2

--- a/solution.py
+++ b/solution.py
@@ -7,9 +7,7 @@
 
 AXES = ("ylo", "zhi", "zlo", "x", "yhi", "core")
 QUARTER = ("ylo", "zhi")
-GRP = ("ylo", "zhi", "zlo", "x")
 FSDP = ("yhi", "core")
-PLANE = ("yhi", "core", "ylo", "x")
 SIZES = (2, 2, 6, 4, 4, 2)
 DEVICES = 768
 N_QUARTER = 4
@@ -103,6 +101,10 @@
         grad_ref[:, at] = (inv * (scaled - unit_ref[:, at] * inner)).astype(BF16)
 
 
+def copy_kernel(in_ref, out_ref):
+    out_ref[...] = in_ref[...]
+
+
 def kernel_call(body, outs, in_specs, cost):
     return pl.pallas_call(
         body,
@@ -121,6 +123,14 @@
 def turned(value, steps):
     pairs = [(source, (source + steps) % N_QUARTER) for source in range(N_QUARTER)]
     return lax.ppermute(value, QUARTER, pairs)
+
+
+def repeated(part, times):
+    return jnp.broadcast_to(part[None], (times, 8, LANES)).reshape(times * 8, LANES)
+
+
+def added(pieces):
+    return jnp.sum(pieces.reshape(-1, 8, LANES), axis=0)
 
 
 def shape(*dims, dtype=F32):
@@ -158,11 +168,14 @@
     )
     vision_grad = turned(grad, -1)
 
-    pieces = exchange(terms, PLANE)
-    part = jnp.sum(pieces, axis=0)
-    parts = exchange(jnp.broadcast_to(part[None, :], (DEVICES // N_FSDP, LANES)), GRP)
-    gain_grad = jnp.sum(parts.reshape(2, 12, 4, LANES), axis=1).reshape(WIDTH // N_FSDP)
-    return (vision_grad, gain_grad)
+    (vision_grad,) = kernel_call(copy_kernel, [shape(VIS, WIDTH, dtype=BF16)], [VMEM], 2**18)(
+        vision_grad
+    )
+
+    part = added(exchange(terms, FSDP))
+    part = added(exchange(repeated(part, 8), ("ylo", "x")))
+    part = added(exchange(repeated(part, 12), ("zhi", "zlo")))
+    return (vision_grad, part.reshape(WIDTH // N_FSDP))
 
 
 def solution(mesh):

time: 111 us -> 114 us (1.027)
  the two profiles are of different devices: /device:TPU:1 before, /device:TPU:16 now
where the time goes in v3:
time: 114 us
  blocking collectives  50.2 us (44%)
  starting transfers between devices  38.8 us (34%)
  waiting for transfers between devices  14.4 us (13%)
  other arithmetic  5.36 us (5%)
  Pallas kernels  2.72 us (2%)
  local copies, waits for them, and re-layouts  1.51 us (1%)
    all_to_all x3, blocking collectives, exchange(): return lax.all_to_all(value, axes, split_axis=0, concat_axis=0, tiled=True)  50.2 us
    all_to_all x2, starting transfers between devices, exchange(): return lax.all_to_all(value, axes, split_axis=0, concat_axis=0, tiled=True)  26.7 us
    all_to_all x2, waiting for transfers between devices, exchange(): return lax.all_to_all(value, axes, split_axis=0, concat_axis=0, tiled=True)  14.4 us
    ppermute x2, starting transfers between devices, turned(): return lax.ppermute(value, QUARTER, pairs)  12.1 us
    reduce_sum x1, other arithmetic, program(): text_terms = jnp.sum(cotangent.astype(F32) * values * kept, axis=0)  2.34 us
  transfers between devices with their start and end apart: 4, of which 2 were waited for; matrix products, arithmetic and copies ran while one was open for 5% of the time, Pallas kernels for 1%

profile of v3, /device:TPU:16, one launch (start us, length us, event | category | flops | bytes accessed | tf_op | source)
XLA Modules:
  0.0 113.8 jit_solution(467366886598564358)
XLA Ops:
  0.6 0.0 copy-start.1
  0.6 0.0 copy-start
  0.7 1.4 %broadcast_in_dim.13 = s32[32,1,16]{2,1,0:T(1,128)} broadcast(s32[16]{0:T(128)} %param.7), dimensions={2} | broadcast | bytes 2112 | tf_op jit(solution)/shard_map/broadcast_in_dim | solution.py:143
  2.1 20.3 %all-to-all-start = ((s32[32,1,16]{2,1,0:T(1,128)}), s32[32,1,16]{2,1,0:T(1,128)S(1)}, u32[]{:S(2)}, u32[]{:S(2)}) async-start(s32[32,1,16]{2,1,0:T(1,128)} %broadcast_in_dim.13), calls=%async_computation | async-start | bytes 32768 | tf_op jit(solution)/shard_map/all_to_all | solution.py:120
  22.3 9.7 %collective-permute-start = (bf16[16,8192]{1,0:T(8,128)(2,1)}, bf16[16,8192]{1,0:T(8,128)(2,1)S(1)}, u32[]{:S(2)}, u32[]{:S(2)}) collective-permute-start(bf16[16,8192]{1,0:T(8,128)(2,1)} %param.6), channel_id=1, source_target_pairs={{0,192},{192,384},{384,576},{576,0},{1,193},{193,385},{385,577},{5... | collective-permute-start | bytes 786440 | tf_op jit(solution)/shard_map/ppermute | solution.py:125
  32.0 2.1 %fusion.2 = f32[128]{0:T(128)S(1)} fusion(bf16[128,8192]{1,0:T(8,128)(2,1)} %param.5), kind=kLoop, calls=%fused_computation.4 | loop fusion | flops 3145600 | bytes 2097664 | tf_op jit(solution)/shard_map/reduce_sum | solution.py:156
  34.1 0.7 all-to-all-done
  34.9 0.0 copy-done.1
  34.9 0.0 copy-done
  34.9 1.5 %shard_map.68 = (bf16[64,4224]{1,0:T(8,128)(2,1)}, bf16[32,64]{1,0:T(8,128)(2,1)S(1)}, f32[8,128]{1,0:T(8,128)S(1)}) custom-call(s32[1]{0:T(128)} %bitcast.dev_ref, s32[32,16]{1,0:T(8,128)S(1)} %bitcast.13, bf16[8,128]{1,0:T(8,128)(2,1)S(1)} %bitcast.15, bf16[128,8192]{1,0:T(8,128)(2,1)S(1)} %copy-done), custom_call_target="tpu_custom_call" | custom-call | flops 2097152 | bytes 2097152 | tf_op jit(solution)/shard_map/pallas_call | solution.py:147
  36.4 6.5 %all-to-all-start.1 = ((bf16[8,8,4224]{2,1,0:T(8,128)(2,1)}), bf16[8,8,4224]{2,1,0:T(8,128)(2,1)S(1)}, u32[]{:S(2)}, u32[]{:S(2)}) async-start(bf16[8,8,4224]{2,1,0:T(8,128)(2,1)} %bitcast.3), calls=%async_computation.1 | async-start | bytes 1081344 | tf_op jit(solution)/shard_map/all_to_all | solution.py:120
  42.9 2.3 %fusion.1 = f32[8192]{0:T(1024)S(1)} fusion(bf16[128,8192]{1,0:T(8,128)(2,1)} %param.5, bf16[128,8192]{1,0:T(8,128)(2,1)S(1)} %copy-done, f32[128]{0:T(128)S(1)} %bitcast_select_fusion), kind=kLoop, calls=%fused_computation.3 | loop fusion | flops 5234688 | bytes 4227584 | tf_op jit(solution)/shard_map/reduce_sum | solution.py:158
  45.2 0.0 collective-permute-done
  45.2 0.2 fusion.3
  45.4 0.1 convert_multiply_fusion.2.unit_ref
  45.5 13.7 %all-to-all-done.1 = bf16[8,8,4224]{2,1,0:T(8,128)(2,1)S(1)} async-done(((bf16[8,8,4224]{2,1,0:T(8,128)(2,1)}), bf16[8,8,4224]{2,1,0:T(8,128)(2,1)S(1)}, u32[]{:S(2)}, u32[]{:S(2)}) %all-to-all-start.1) | async-done | bytes 540704 | tf_op jit(solution)/shard_map/all_to_all | solution.py:120
  59.2 0.3 shard_map.69
  59.5 0.1 broadcast_in_dim.14.inv_ref
  59.5 0.3 shard_map.70
  59.8 2.4 %collective-permute-start.1 = (bf16[16,8192]{1,0:T(8,128)(2,1)S(1)}, bf16[16,8192]{1,0:T(8,128)(2,1)S(1)}, u32[]{:S(2)}, u32[]{:S(2)}) collective-permute-start(bf16[16,8192]{1,0:T(8,128)(2,1)S(1)} %shard_map.70), channel_id=1, source_target_pairs={{0,576},{192,0},{384,192},{576,384},{1,577},{193,1},{385,193},{577... | collective-permute-start | bytes 786440 | tf_op jit(solution)/shard_map/ppermute | solution.py:125
  62.2 10.4 %all_to_all.40 = f32[8,8,128]{2,1,0:T(8,128)S(1)} all-to-all(f32[8,8,128]{2,1,0:T(8,128)S(1)} %bitcast.14), channel_id=1, replica_groups=mesh['ylo'=2,'zhi'=2,'zlo'=6,'x'=4,'yhi'=4,'core'=2] {'yhi','core'}, dimensions={0} | all-to-all | bytes 65536 | tf_op jit(solution)/shard_map/all_to_all | solution.py:120
  72.6 11.2 %all_to_all.41 = f32[8,8,128]{2,1,0:T(8,128)S(1)} all-to-all(f32[8,8,128]{2,1,0:T(8,128)S(1)} %broadcast_in_dim.15), channel_id=1, replica_groups=mesh['ylo'=2,'zhi'=2,'zlo'=6,'x'=4,'yhi'=4,'core'=2] {'ylo','x'}, dimensions={0} | all-to-all | bytes 65536 | tf_op jit(solution)/shard_map/all_to_all | solution.py:120
  83.9 28.6 %all_to_all.42 = f32[12,8,128]{2,1,0:T(8,128)S(1)} all-to-all(f32[12,8,128]{2,1,0:T(8,128)S(1)} %broadcast_in_dim.16), channel_id=1, replica_groups=mesh['ylo'=2,'zhi'=2,'zlo'=6,'x'=4,'yhi'=4,'core'=2] {'zhi','zlo'}, dimensions={0} | all-to-all | bytes 98304 | tf_op jit(solution)/shard_map/all_to_all | solution.py:120
  112.5 0.6 reduce_sum.59
  113.1 0.0 collective-permute-done.1.in_ref
  113.1 0.7 shard_map.71
  (6 shorter events, 0.0 us)
Async XLA Ops:
  0.6 34.3 %copy-start.1 = (bf16[1024]{0:T(1024)(128)(2,1)S(1)}, bf16[1024]{0:T(1024)(128)(2,1)}, u32[]{:S(2)}) copy-start(bf16[1024]{0:T(1024)(128)(2,1)} %param.8) | copy-start | bytes 6148
  0.6 34.2 %copy-start = (bf16[128,8192]{1,0:T(8,128)(2,1)S(1)}, bf16[128,8192]{1,0:T(8,128)(2,1)}, u32[]{:S(2)}) copy-start(bf16[128,8192]{1,0:T(8,128)(2,1)} %cot_ref.1) | copy-start | bytes 6291460
  2.1 32.8 %all-to-all-start = ((s32[32,1,16]{2,1,0:T(1,128)}), s32[32,1,16]{2,1,0:T(1,128)S(1)}, u32[]{:S(2)}, u32[]{:S(2)}) async-start(s32[32,1,16]{2,1,0:T(1,128)} %broadcast_in_dim.13), calls=%async_computation | async-start | bytes 32768 | tf_op jit(solution)/shard_map/all_to_all | solution.py:120
  22.3 22.9 %collective-permute-start = (bf16[16,8192]{1,0:T(8,128)(2,1)}, bf16[16,8192]{1,0:T(8,128)(2,1)S(1)}, u32[]{:S(2)}, u32[]{:S(2)}) collective-permute-start(bf16[16,8192]{1,0:T(8,128)(2,1)} %param.6), channel_id=1, source_target_pairs={{0,192},{192,384},{384,576},{576,0},{1,193},{193,385},{385,577},{5... | collective-permute-start | bytes 786440 | tf_op jit(solution)/shard_map/ppermute | solution.py:125
  36.4 22.8 %all-to-all-start.1 = ((bf16[8,8,4224]{2,1,0:T(8,128)(2,1)}), bf16[8,8,4224]{2,1,0:T(8,128)(2,1)S(1)}, u32[]{:S(2)}, u32[]{:S(2)}) async-start(bf16[8,8,4224]{2,1,0:T(8,128)(2,1)} %bitcast.3), calls=%async_computation.1 | async-start | bytes 1081344 | tf_op jit(solution)/shard_map/all_to_all | solution.py:120
  59.8 53.3 %collective-permute-start.1 = (bf16[16,8192]{1,0:T(8,128)(2,1)S(1)}, bf16[16,8192]{1,0:T(8,128)(2,1)S(1)}, u32[]{:S(2)}, u32[]{:S(2)}) collective-permute-start(bf16[16,8192]{1,0:T(8,128)(2,1)S(1)} %shard_map.70), channel_id=1, source_target_pairs={{0,576},{192,0},{384,192},{576,384},{1,577},{193,1},{385,193},{577... | collective-permute-start | bytes 786440 | tf_op jit(solution)/shard_map/ppermute | solution.py:125

commit v4 on v3

--- a/solution.py
+++ b/solution.py
@@ -20,6 +20,7 @@
 LANES = 128
 SLOTS = N_FSDP * 2 * CAP
 BLOCKS = WIDTH // LANES
+FIRST = 6144
 F32 = jnp.float32
 BF16 = jnp.bfloat16
 VMEM = pl.BlockSpec(memory_space=pltpu.VMEM)
@@ -86,7 +87,7 @@
         terms_ref[block : block + 8, :] = text_ref[block : block + 8, :] + jnp.concatenate(rows, axis=0)
 
 
-def grads_kernel(arrived_ref, upper_ref, unit_ref, inv_ref, grad_ref):
+def grads_kernel(arrived_ref, upper_ref, unit_ref, inv_ref, first_ref, last_ref):
     total = jnp.zeros((VIS, LANES), F32)
     for b in range(BLOCKS):
         at = slice(b * LANES, (b + 1) * LANES)
@@ -98,11 +99,24 @@
         at = slice(b * LANES, (b + 1) * LANES)
         gain = arrived_ref[b : b + 1, HALF:].astype(F32)
         scaled = upper_ref[:, at].astype(F32) * gain
-        grad_ref[:, at] = (inv * (scaled - unit_ref[:, at] * inner)).astype(BF16)
-
-
-def copy_kernel(in_ref, out_ref):
-    out_ref[...] = in_ref[...]
+        grad = (inv * (scaled - unit_ref[:, at] * inner)).astype(BF16)
+        if b * LANES < FIRST:
+            first_ref[:, at] = grad
+        else:
+            last_ref[:, b * LANES - FIRST : (b + 1) * LANES - FIRST] = grad
+
+
+def repeat_kernel(tok_ref, out_ref):
+    out_ref[...] = jnp.broadcast_to(tok_ref[...], out_ref.shape)
+
+
+def finish_kernel(pieces_ref, first_ref, last_ref, grad_ref, sum_ref):
+    grad_ref[:, :FIRST] = first_ref[...]
+    grad_ref[:, FIRST:] = last_ref[...]
+    total = pieces_ref[:8, :]
+    for k in range(1, 12):
+        total = total + pieces_ref[8 * k : 8 * k + 8, :]
+    sum_ref[...] = total
 
 
 def kernel_call(body, outs, in_specs, cost):
@@ -139,9 +153,10 @@
 
 def program(text, vision, vision_token, gain, cotangent):
     device = jnp.full((1,), lax.axis_index(AXES), jnp.int32)
-    tokens = exchange(
-        jnp.broadcast_to(vision_token[None, :], (N_QUARTER * N_FSDP, VIS)), QUARTER + FSDP
-    )
+    (asked,) = kernel_call(
+        repeat_kernel, [shape(N_QUARTER * N_FSDP, VIS, dtype=jnp.int32)], [VMEM], 2**12
+    )(vision_token.reshape(1, VIS))
+    tokens = exchange(asked, QUARTER + FSDP)
     rows = turned(vision, 1)
 
     sent, order, taken = kernel_call(
@@ -163,19 +178,22 @@
     terms, upper = kernel_call(
         terms_kernel, [shape(BLOCKS, LANES), shape(VIS, WIDTH, dtype=BF16)], [VMEM] * 4, 2**20
     )(order, arrived, unit, text_terms.reshape(BLOCKS, LANES))
-    (grad,) = kernel_call(grads_kernel, [shape(VIS, WIDTH, dtype=BF16)], [VMEM] * 4, 2**20)(
-        arrived, upper, unit, jnp.broadcast_to(inv_v, (VIS, LANES))
-    )
-    vision_grad = turned(grad, -1)
-
-    (vision_grad,) = kernel_call(copy_kernel, [shape(VIS, WIDTH, dtype=BF16)], [VMEM], 2**18)(
-        vision_grad
-    )
+    first, last = kernel_call(
+        grads_kernel,
+        [shape(VIS, FIRST, dtype=BF16), shape(VIS, WIDTH - FIRST, dtype=BF16)],
+        [VMEM] * 4,
+        2**20,
+    )(arrived, upper, unit, jnp.broadcast_to(inv_v, (VIS, LANES)))
+    first = turned(first, -1)
+    last = turned(last, -1)
 
     part = added(exchange(terms, FSDP))
     part = added(exchange(repeated(part, 8), ("ylo", "x")))
-    part = added(exchange(repeated(part, 12), ("zhi", "zlo")))
-    return (vision_grad, part.reshape(WIDTH // N_FSDP))
+    pieces = exchange(repeated(part, 12), ("zhi", "zlo"))
+    vision_grad, gain_grad = kernel_call(
+        finish_kernel, [shape(VIS, WIDTH, dtype=BF16), shape(8, LANES)], [VMEM] * 3, 2**19
+    )(pieces, first, last)
+    return (vision_grad, gain_grad.reshape(WIDTH // N_FSDP))
 
 
 def solution(mesh):

time: 114 us -> 111 us (0.974)
  the two profiles are of different devices: /device:TPU:16 before, /device:TPU:1 now
where the time goes in v4:
time: 111 us; the launch traced here: 109 us
  starting transfers between devices  67.5 us (61%)
  waiting for transfers between devices  21.2 us (19%)
  blocking collectives  9.11 us (8%)
  other arithmetic  4.75 us (4%)
  Pallas kernels  3.95 us (4%)
  local copies, waits for them, and re-layouts  1.51 us (1%)
    all_to_all x4, starting transfers between devices, exchange(): return lax.all_to_all(value, axes, split_axis=0, concat_axis=0, tiled=True)  44.6 us
    ppermute x3, starting transfers between devices, turned(): return lax.ppermute(value, QUARTER, pairs)  22.9 us
    all_to_all x4, waiting for transfers between devices, exchange(): return lax.all_to_all(value, axes, split_axis=0, concat_axis=0, tiled=True)  18.5 us
    all_to_all x1, blocking collectives, exchange(): return lax.all_to_all(value, axes, split_axis=0, concat_axis=0, tiled=True)  9.11 us
    ppermute x3, waiting for transfers between devices, turned(): return lax.ppermute(value, QUARTER, pairs)  2.67 us
    reduce_sum x1, other arithmetic, program(): text_terms = jnp.sum(cotangent.astype(F32) * values * kept, axis=0)  2.34 us
  transfers between devices with their start and end apart: 7, of which 4 were waited for; matrix products, arithmetic and copies ran while one was open for 5% of the time, Pallas kernels for 2%

profile of v4, /device:TPU:1, one launch (start us, length us, event | category | flops | bytes accessed | tf_op | source)
XLA Modules:
  0.0 108.8 jit_solution(5601191266058770918)
XLA Ops:
  0.6 0.0 copy-start.1
  0.6 0.0 copy-start
  0.7 0.0 copy-start.2
  0.7 0.8 copy-done.2
  1.5 0.6 shard_map.68
  2.1 21.4 %all-to-all-start = ((s32[32,1,16]{2,1,0:T(1,128)}), s32[32,1,16]{2,1,0:T(1,128)S(1)}, u32[]{:S(2)}, u32[]{:S(2)}) async-start(s32[32,1,16]{2,1,0:T(1,128)} %bitcast.3), calls=%async_computation | async-start | bytes 32768 | tf_op jit(solution)/shard_map/all_to_all | solution.py:134
  23.5 9.6 %collective-permute-start = (bf16[16,8192]{1,0:T(8,128)(2,1)}, bf16[16,8192]{1,0:T(8,128)(2,1)S(1)}, u32[]{:S(2)}, u32[]{:S(2)}) collective-permute-start(bf16[16,8192]{1,0:T(8,128)(2,1)} %param.6), channel_id=1, source_target_pairs={{0,192},{192,384},{384,576},{576,0},{1,193},{193,385},{385,577},{5... | collective-permute-start | bytes 786440 | tf_op jit(solution)/shard_map/ppermute | solution.py:139
  33.1 2.1 %fusion.2 = f32[128]{0:T(128)S(1)} fusion(bf16[128,8192]{1,0:T(8,128)(2,1)} %param.5), kind=kLoop, calls=%fused_computation.4 | loop fusion | flops 3145600 | bytes 2097664 | tf_op jit(solution)/shard_map/reduce_sum | solution.py:171
  35.2 2.4 %all-to-all-done = s32[32,1,16]{2,1,0:T(1,128)S(1)} async-done(((s32[32,1,16]{2,1,0:T(1,128)}), s32[32,1,16]{2,1,0:T(1,128)S(1)}, u32[]{:S(2)}, u32[]{:S(2)}) %all-to-all-start) | async-done | bytes 2080 | tf_op jit(solution)/shard_map/all_to_all | solution.py:134
  37.6 0.0 copy-done.1
  37.6 0.0 copy-done
  37.6 1.5 %shard_map.69 = (bf16[64,4224]{1,0:T(8,128)(2,1)}, bf16[32,64]{1,0:T(8,128)(2,1)S(1)}, f32[8,128]{1,0:T(8,128)S(1)}) custom-call(s32[1]{0:T(128)} %bitcast.dev_ref, s32[32,16]{1,0:T(8,128)S(1)} %bitcast.19, bf16[8,128]{1,0:T(8,128)(2,1)S(1)} %bitcast.20, bf16[128,8192]{1,0:T(8,128)(2,1)S(1)} %copy-done), custom_call_target="tpu_custom_call" | custom-call | flops 2097152 | bytes 2097152 | tf_op jit(solution)/shard_map/pallas_call | solution.py:162
  39.1 4.9 %all-to-all-start.1 = ((bf16[8,8,4224]{2,1,0:T(8,128)(2,1)}), bf16[8,8,4224]{2,1,0:T(8,128)(2,1)S(1)}, u32[]{:S(2)}, u32[]{:S(2)}) async-start(bf16[8,8,4224]{2,1,0:T(8,128)(2,1)} %bitcast.6), calls=%async_computation.1 | async-start | bytes 1081344 | tf_op jit(solution)/shard_map/all_to_all | solution.py:134
  44.0 2.3 %fusion.1 = f32[8192]{0:T(1024)S(1)} fusion(bf16[128,8192]{1,0:T(8,128)(2,1)} %param.5, bf16[128,8192]{1,0:T(8,128)(2,1)S(1)} %copy-done, f32[128]{0:T(128)S(1)} %bitcast_select_fusion), kind=kLoop, calls=%fused_computation.3 | loop fusion | flops 5234688 | bytes 4227584 | tf_op jit(solution)/shard_map/reduce_sum | solution.py:173
  46.4 0.0 collective-permute-done
  46.4 0.2 fusion.3
  46.6 0.1 convert_multiply_fusion.2.unit_ref
  46.7 12.9 %all-to-all-done.1 = bf16[8,8,4224]{2,1,0:T(8,128)(2,1)S(1)} async-done(((bf16[8,8,4224]{2,1,0:T(8,128)(2,1)}), bf16[8,8,4224]{2,1,0:T(8,128)(2,1)S(1)}, u32[]{:S(2)}, u32[]{:S(2)}) %all-to-all-start.1) | async-done | bytes 540704 | tf_op jit(solution)/shard_map/all_to_all | solution.py:134
  59.6 0.9 shard_map.70
  60.5 5.0 %all-to-all-start.2 = ((f32[8,8,128]{2,1,0:T(8,128)}), f32[8,8,128]{2,1,0:T(8,128)S(1)}, u32[]{:S(2)}, u32[]{:S(2)}) async-start(f32[8,8,128]{2,1,0:T(8,128)} %bitcast.10), calls=%async_computation.2 | async-start | bytes 65536 | tf_op jit(solution)/shard_map/all_to_all | solution.py:134
  65.5 0.1 broadcast_in_dim.13.inv_ref
  65.5 0.2 shard_map.71
  65.8 3.6 %collective-permute-start.1 = (bf16[16,6144]{1,0:T(8,128)(2,1)S(1)}, bf16[16,6144]{1,0:T(8,128)(2,1)S(1)}, u32[]{:S(2)}, u32[]{:S(2)}) collective-permute-start(bf16[16,6144]{1,0:T(8,128)(2,1)S(1)} %get-tuple-element.16), channel_id=1, source_target_pairs={{0,576},{192,0},{384,192},{576,384},{1,577},{193,1},{385,193},{577... | collective-permute-start | bytes 589832 | tf_op jit(solution)/shard_map/ppermute | solution.py:139
  69.4 3.2 %all-to-all-done.2 = f32[8,8,128]{2,1,0:T(8,128)S(1)} async-done(((f32[8,8,128]{2,1,0:T(8,128)}), f32[8,8,128]{2,1,0:T(8,128)S(1)}, u32[]{:S(2)}, u32[]{:S(2)}) %all-to-all-start.2) | async-done | bytes 32800 | tf_op jit(solution)/shard_map/all_to_all | solution.py:134
  72.6 9.1 %all_to_all.45 = f32[8,8,128]{2,1,0:T(8,128)S(1)} all-to-all(f32[8,8,128]{2,1,0:T(8,128)S(1)} %broadcast_in_dim.11), channel_id=1, replica_groups=mesh['ylo'=2,'zhi'=2,'zlo'=6,'x'=4,'yhi'=4,'core'=2] {'ylo','x'}, dimensions={0} | all-to-all | bytes 65536 | tf_op jit(solution)/shard_map/all_to_all | solution.py:134
  81.7 0.6 broadcast_in_dim.12
  82.4 13.3 %all-to-all-start.4 = ((f32[12,8,128]{2,1,0:T(8,128)}), f32[12,8,128]{2,1,0:T(8,128)S(1)}, u32[]{:S(2)}, u32[]{:S(2)}) async-start(f32[12,8,128]{2,1,0:T(8,128)} %broadcast_in_dim.12), calls=%async_computation.4 | async-start | bytes 98304 | tf_op jit(solution)/shard_map/all_to_all | solution.py:134
  95.7 9.7 %collective-permute-start.2 = (bf16[16,2048]{1,0:T(8,128)(2,1)S(1)}, bf16[16,2048]{1,0:T(8,128)(2,1)S(1)}, u32[]{:S(2)}, u32[]{:S(2)}) collective-permute-start(bf16[16,2048]{1,0:T(8,128)(2,1)S(1)} %get-tuple-element.17), channel_id=1, source_target_pairs={{0,576},{192,0},{384,192},{576,384},{1,577},{193,1},{385,193},{577... | collective-permute-start | bytes 196616 | tf_op jit(solution)/shard_map/ppermute | solution.py:139
  105.4 2.7 %collective-permute-done.2.last_ref = bf16[16,2048]{1,0:T(8,128)(2,1)S(1)} collective-permute-done((bf16[16,2048]{1,0:T(8,128)(2,1)S(1)}, bf16[16,2048]{1,0:T(8,128)(2,1)S(1)}, u32[]{:S(2)}, u32[]{:S(2)}) %collective-permute-start.2) | collective-permute-done | bytes 65568 | tf_op jit(solution)/shard_map/ppermute | solution.py:139
  108.0 0.0 collective-permute-done.1.first_ref
  108.0 0.0 all-to-all-done.4
  108.0 0.7 shard_map.72
  (5 shorter events, 0.0 us)
Async XLA Ops:
  0.6 37.0 %copy-start.1 = (bf16[1024]{0:T(1024)(128)(2,1)S(1)}, bf16[1024]{0:T(1024)(128)(2,1)}, u32[]{:S(2)}) copy-start(bf16[1024]{0:T(1024)(128)(2,1)} %param.8) | copy-start | bytes 6148
  0.6 37.0 %copy-start = (bf16[128,8192]{1,0:T(8,128)(2,1)S(1)}, bf16[128,8192]{1,0:T(8,128)(2,1)}, u32[]{:S(2)}) copy-start(bf16[128,8192]{1,0:T(8,128)(2,1)} %cot_ref.1) | copy-start | bytes 6291460
  0.7 0.8 copy-start.2
  2.1 35.5 %all-to-all-start = ((s32[32,1,16]{2,1,0:T(1,128)}), s32[32,1,16]{2,1,0:T(1,128)S(1)}, u32[]{:S(2)}, u32[]{:S(2)}) async-start(s32[32,1,16]{2,1,0:T(1,128)} %bitcast.3), calls=%async_computation | async-start | bytes 32768 | tf_op jit(solution)/shard_map/all_to_all | solution.py:134
  23.5 22.9 %collective-permute-start = (bf16[16,8192]{1,0:T(8,128)(2,1)}, bf16[16,8192]{1,0:T(8,128)(2,1)S(1)}, u32[]{:S(2)}, u32[]{:S(2)}) collective-permute-start(bf16[16,8192]{1,0:T(8,128)(2,1)} %param.6), channel_id=1, source_target_pairs={{0,192},{192,384},{384,576},{576,0},{1,193},{193,385},{385,577},{5... | collective-permute-start | bytes 786440 | tf_op jit(solution)/shard_map/ppermute | solution.py:139
  39.1 20.5 %all-to-all-start.1 = ((bf16[8,8,4224]{2,1,0:T(8,128)(2,1)}), bf16[8,8,4224]{2,1,0:T(8,128)(2,1)S(1)}, u32[]{:S(2)}, u32[]{:S(2)}) async-start(bf16[8,8,4224]{2,1,0:T(8,128)(2,1)} %bitcast.6), calls=%async_computation.1 | async-start | bytes 1081344 | tf_op jit(solution)/shard_map/all_to_all | solution.py:134
  60.5 12.1 %all-to-all-start.2 = ((f32[8,8,128]{2,1,0:T(8,128)}), f32[8,8,128]{2,1,0:T(8,128)S(1)}, u32[]{:S(2)}, u32[]{:S(2)}) async-start(f32[8,8,128]{2,1,0:T(8,128)} %bitcast.10), calls=%async_computation.2 | async-start | bytes 65536 | tf_op jit(solution)/shard_map/all_to_all | solution.py:134
  65.8 42.3 %collective-permute-start.1 = (bf16[16,6144]{1,0:T(8,128)(2,1)S(1)}, bf16[16,6144]{1,0:T(8,128)(2,1)S(1)}, u32[]{:S(2)}, u32[]{:S(2)}) collective-permute-start(bf16[16,6144]{1,0:T(8,128)(2,1)S(1)} %get-tuple-element.16), channel_id=1, source_target_pairs={{0,576},{192,0},{384,192},{576,384},{1,577},{193,1},{385,193},{577... | collective-permute-start | bytes 589832 | tf_op jit(solution)/shard_map/ppermute | solution.py:139
  82.4 25.7 %all-to-all-start.4 = ((f32[12,8,128]{2,1,0:T(8,128)}), f32[12,8,128]{2,1,0:T(8,128)S(1)}, u32[]{:S(2)}, u32[]{:S(2)}) async-start(f32[12,8,128]{2,1,0:T(8,128)} %broadcast_in_dim.12), calls=%async_computation.4 | async-start | bytes 98304 | tf_op jit(solution)/shard_map/all_to_all | solution.py:134
  95.7 12.4 %collective-permute-start.2 = (bf16[16,2048]{1,0:T(8,128)(2,1)S(1)}, bf16[16,2048]{1,0:T(8,128)(2,1)S(1)}, u32[]{:S(2)}, u32[]{:S(2)}) collective-permute-start(bf16[16,2048]{1,0:T(8,128)(2,1)S(1)} %get-tuple-element.17), channel_id=1, source_target_pairs={{0,576},{192,0},{384,192},{576,384},{1,577},{193,1},{385,193},{577... | collective-permute-start | bytes 196616 | tf_op jit(solution)/shard_map/ppermute | solution.py:139

commit v5 on v2

--- a/solution.py
+++ b/solution.py
@@ -103,6 +103,15 @@
         grad_ref[:, at] = (inv * (scaled - unit_ref[:, at] * inner)).astype(BF16)
 
 
+def finish_kernel(parts_ref, rows_ref, grad_ref, sum_ref):
+    grad_ref[...] = rows_ref[...]
+    for low in range(2):
+        total = parts_ref[low * 48 : low * 48 + 4, :]
+        for z in range(1, 12):
+            total = total + parts_ref[low * 48 + 4 * z : low * 48 + 4 * z + 4, :]
+        sum_ref[4 * low : 4 * low + 4, :] = total
+
+
 def kernel_call(body, outs, in_specs, cost):
     return pl.pallas_call(
         body,
@@ -161,8 +170,10 @@
     pieces = exchange(terms, PLANE)
     part = jnp.sum(pieces, axis=0)
     parts = exchange(jnp.broadcast_to(part[None, :], (DEVICES // N_FSDP, LANES)), GRP)
-    gain_grad = jnp.sum(parts.reshape(2, 12, 4, LANES), axis=1).reshape(WIDTH // N_FSDP)
-    return (vision_grad, gain_grad)
+    vision_grad, gain_grad = kernel_call(
+        finish_kernel, [shape(VIS, WIDTH, dtype=BF16), shape(8, LANES)], [VMEM] * 2, 2**19
+    )(parts, vision_grad)
+    return (vision_grad, gain_grad.reshape(WIDTH // N_FSDP))
 
 
 def solution(mesh):

time: 111 us -> 110 us (level)
  transfers between devices with their start and end apart: 4 -> 4, of which waited for: 2 -> 2; matrix products, arithmetic and copies ran while one was open for 5% -> 4% of each run, Pallas kernels for 1% -> 1%
where the time goes in v5:
time: 110 us
  blocking collectives  44.3 us (40%)
  starting transfers between devices  40.2 us (37%)
  waiting for transfers between devices  15.3 us (14%)
  other arithmetic  4.82 us (4%)
  Pallas kernels  2.72 us (2%)
  local copies, waits for them, and re-layouts  1.53 us (1%)
    all_to_all x2, blocking collectives, exchange(): return lax.all_to_all(value, axes, split_axis=0, concat_axis=0, tiled=True)  44.3 us
    all_to_all x2, starting transfers between devices, exchange(): return lax.all_to_all(value, axes, split_axis=0, concat_axis=0, tiled=True)  26.3 us
    all_to_all x2, waiting for transfers between devices, exchange(): return lax.all_to_all(value, axes, split_axis=0, concat_axis=0, tiled=True)  15.3 us
    ppermute x2, starting transfers between devices, turned(): return lax.ppermute(value, QUARTER, pairs)  13.9 us
    reduce_sum x1, other arithmetic, program(): text_terms = jnp.sum(cotangent.astype(F32) * values * kept, axis=0)  2.34 us
  transfers between devices with their start and end apart: 4, of which 2 were waited for; matrix products, arithmetic and copies ran while one was open for 4% of the time, Pallas kernels for 1%

profile of v5, /device:TPU:1, one launch (start us, length us, event | category | flops | bytes accessed | tf_op | source)
XLA Modules:
  0.0 109.7 jit_solution(5563673092129483840)
XLA Ops:
  0.6 0.0 copy-start.1
  0.6 0.0 copy-start
  0.7 1.4 %broadcast_in_dim.11 = s32[32,1,16]{2,1,0:T(1,128)} broadcast(s32[16]{0:T(128)} %param.7), dimensions={2} | broadcast | bytes 2112 | tf_op jit(solution)/shard_map/broadcast_in_dim | solution.py:142
  2.1 21.4 %all-to-all-start = ((s32[32,1,16]{2,1,0:T(1,128)}), s32[32,1,16]{2,1,0:T(1,128)S(1)}, u32[]{:S(2)}, u32[]{:S(2)}) async-start(s32[32,1,16]{2,1,0:T(1,128)} %broadcast_in_dim.11), calls=%async_computation | async-start | bytes 32768 | tf_op jit(solution)/shard_map/all_to_all | solution.py:127
  23.5 9.6 %collective-permute-start = (bf16[16,8192]{1,0:T(8,128)(2,1)}, bf16[16,8192]{1,0:T(8,128)(2,1)S(1)}, u32[]{:S(2)}, u32[]{:S(2)}) collective-permute-start(bf16[16,8192]{1,0:T(8,128)(2,1)} %param.6), channel_id=1, source_target_pairs={{0,192},{192,384},{384,576},{576,0},{1,193},{193,385},{385,577},{5... | collective-permute-start | bytes 786440 | tf_op jit(solution)/shard_map/ppermute | solution.py:132
  33.1 2.1 %fusion.2 = f32[128]{0:T(128)S(1)} fusion(bf16[128,8192]{1,0:T(8,128)(2,1)} %param.5), kind=kLoop, calls=%fused_computation.4 | loop fusion | flops 3145600 | bytes 2097664 | tf_op jit(solution)/shard_map/reduce_sum | solution.py:155
  35.2 2.4 %all-to-all-done = s32[32,1,16]{2,1,0:T(1,128)S(1)} async-done(((s32[32,1,16]{2,1,0:T(1,128)}), s32[32,1,16]{2,1,0:T(1,128)S(1)}, u32[]{:S(2)}, u32[]{:S(2)}) %all-to-all-start) | async-done | bytes 2080 | tf_op jit(solution)/shard_map/all_to_all | solution.py:127
  37.6 0.0 copy-done.1
  37.6 0.0 copy-done
  37.6 1.5 %shard_map.68 = (bf16[64,4224]{1,0:T(8,128)(2,1)}, bf16[32,64]{1,0:T(8,128)(2,1)S(1)}, f32[8,128]{1,0:T(8,128)S(1)}) custom-call(s32[1]{0:T(128)} %bitcast.dev_ref, s32[32,16]{1,0:T(8,128)S(1)} %bitcast.17, bf16[8,128]{1,0:T(8,128)(2,1)S(1)} %bitcast.19, bf16[128,8192]{1,0:T(8,128)(2,1)S(1)} %copy-done), custom_call_target="tpu_custom_call" | custom-call | flops 2097152 | bytes 2097152 | tf_op jit(solution)/shard_map/pallas_call | solution.py:146
  39.1 4.9 %all-to-all-start.1 = ((bf16[8,8,4224]{2,1,0:T(8,128)(2,1)}), bf16[8,8,4224]{2,1,0:T(8,128)(2,1)S(1)}, u32[]{:S(2)}, u32[]{:S(2)}) async-start(bf16[8,8,4224]{2,1,0:T(8,128)(2,1)} %bitcast.3), calls=%async_computation.1 | async-start | bytes 1081344 | tf_op jit(solution)/shard_map/all_to_all | solution.py:127
  44.0 2.3 %fusion.1 = f32[8192]{0:T(1024)S(1)} fusion(bf16[128,8192]{1,0:T(8,128)(2,1)} %param.5, bf16[128,8192]{1,0:T(8,128)(2,1)S(1)} %copy-done, f32[128]{0:T(128)S(1)} %bitcast_select_fusion), kind=kLoop, calls=%fused_computation.3 | loop fusion | flops 5234688 | bytes 4227584 | tf_op jit(solution)/shard_map/reduce_sum | solution.py:157
  46.4 0.0 collective-permute-done
  46.4 0.2 fusion.3
  46.6 0.1 convert_multiply_fusion.2.unit_ref
  46.7 12.9 %all-to-all-done.1 = bf16[8,8,4224]{2,1,0:T(8,128)(2,1)S(1)} async-done(((bf16[8,8,4224]{2,1,0:T(8,128)(2,1)}), bf16[8,8,4224]{2,1,0:T(8,128)(2,1)S(1)}, u32[]{:S(2)}, u32[]{:S(2)}) %all-to-all-start.1) | async-done | bytes 540704 | tf_op jit(solution)/shard_map/all_to_all | solution.py:127
  59.6 0.3 shard_map.69
  59.9 0.1 broadcast_in_dim.13.inv_ref
  59.9 0.3 shard_map.70
  60.2 4.3 %collective-permute-start.1 = (bf16[16,8192]{1,0:T(8,128)(2,1)S(1)}, bf16[16,8192]{1,0:T(8,128)(2,1)S(1)}, u32[]{:S(2)}, u32[]{:S(2)}) collective-permute-start(bf16[16,8192]{1,0:T(8,128)(2,1)S(1)} %shard_map.70), channel_id=1, source_target_pairs={{0,576},{192,0},{384,192},{576,384},{1,577},{193,1},{385,193},{577... | collective-permute-start | bytes 786440 | tf_op jit(solution)/shard_map/ppermute | solution.py:132
  64.5 16.1 %all_to_all.36 = f32[64,1,128]{2,1,0:T(1,128)S(1)} all-to-all(f32[64,1,128]{2,1,0:T(1,128)S(1)} %bitcast.18), channel_id=1, replica_groups=mesh['ylo'=2,'zhi'=2,'zlo'=6,'x'=4,'yhi'=4,'core'=2] {'yhi','core','ylo'..., dimensions={0} | all-to-all | bytes 65536 | tf_op jit(solution)/shard_map/all_to_all | solution.py:127
  80.6 0.1 reduce_sum.39
  80.7 28.2 %all_to_all.37 = f32[96,1,128]{2,1,0:T(1,128)S(1)} all-to-all(f32[96,1,128]{2,1,0:T(1,128)S(1)} %broadcast_in_dim.12), channel_id=1, replica_groups=mesh['ylo'=2,'zhi'=2,'zlo'=6,'x'=4,'yhi'=4,'core'=2] {'ylo','zhi','zlo',..., dimensions={0} | all-to-all | bytes 98304 | tf_op jit(solution)/shard_map/all_to_all | solution.py:127
  109.0 0.0 collective-permute-done.1.rows_ref
  109.0 0.7 shard_map.71
  (3 shorter events, 0.0 us)
Async XLA Ops:
  0.6 37.0 %copy-start.1 = (bf16[1024]{0:T(1024)(128)(2,1)S(1)}, bf16[1024]{0:T(1024)(128)(2,1)}, u32[]{:S(2)}) copy-start(bf16[1024]{0:T(1024)(128)(2,1)} %param.8) | copy-start | bytes 6148
  0.6 37.0 %copy-start = (bf16[128,8192]{1,0:T(8,128)(2,1)S(1)}, bf16[128,8192]{1,0:T(8,128)(2,1)}, u32[]{:S(2)}) copy-start(bf16[128,8192]{1,0:T(8,128)(2,1)} %cot_ref.1) | copy-start | bytes 6291460
  2.1 35.5 %all-to-all-start = ((s32[32,1,16]{2,1,0:T(1,128)}), s32[32,1,16]{2,1,0:T(1,128)S(1)}, u32[]{:S(2)}, u32[]{:S(2)}) async-start(s32[32,1,16]{2,1,0:T(1,128)} %broadcast_in_dim.11), calls=%async_computation | async-start | bytes 32768 | tf_op jit(solution)/shard_map/all_to_all | solution.py:127
  23.5 22.9 %collective-permute-start = (bf16[16,8192]{1,0:T(8,128)(2,1)}, bf16[16,8192]{1,0:T(8,128)(2,1)S(1)}, u32[]{:S(2)}, u32[]{:S(2)}) collective-permute-start(bf16[16,8192]{1,0:T(8,128)(2,1)} %param.6), channel_id=1, source_target_pairs={{0,192},{192,384},{384,576},{576,0},{1,193},{193,385},{385,577},{5... | collective-permute-start | bytes 786440 | tf_op jit(solution)/shard_map/ppermute | solution.py:132
  39.1 20.5 %all-to-all-start.1 = ((bf16[8,8,4224]{2,1,0:T(8,128)(2,1)}), bf16[8,8,4224]{2,1,0:T(8,128)(2,1)S(1)}, u32[]{:S(2)}, u32[]{:S(2)}) async-start(bf16[8,8,4224]{2,1,0:T(8,128)(2,1)} %bitcast.3), calls=%async_computation.1 | async-start | bytes 1081344 | tf_op jit(solution)/shard_map/all_to_all | solution.py:127
  60.2 48.8 %collective-permute-start.1 = (bf16[16,8192]{1,0:T(8,128)(2,1)S(1)}, bf16[16,8192]{1,0:T(8,128)(2,1)S(1)}, u32[]{:S(2)}, u32[]{:S(2)}) collective-permute-start(bf16[16,8192]{1,0:T(8,128)(2,1)S(1)} %shard_map.70), channel_id=1, source_target_pairs={{0,576},{192,0},{384,192},{576,384},{1,577},{193,1},{385,193},{577... | collective-permute-start | bytes 786440 | tf_op jit(solution)/shard_map/ppermute | solution.py:132

commit v6 on v5

--- a/solution.py
+++ b/solution.py
@@ -38,8 +38,7 @@
 
 def pack_kernel(dev_ref, tok_ref, gain_ref, cot_ref, sent_ref, order_ref, taken_ref):
     dev = dev_ref[0]
-    source = lax.rem(dev // (DEVICES // N_QUARTER) + N_QUARTER - 1, N_QUARTER) * N_FSDP
-    tokens = tok_ref[pl.ds(pl.multiple_of(source, N_FSDP), N_FSDP), :]
+    tokens = tok_ref[...]
     position = dev * TOK + iota((N_FSDP, TOK), 1)
     count = jnp.zeros((N_FSDP, TOK), jnp.int32)
     chosen = [jnp.zeros((N_FSDP, TOK), F32)] * CAP
@@ -64,7 +63,7 @@
         sent_ref[:, k : k + step] = dot(lhs, rhs).astype(BF16)
     gain = gain_ref[...].astype(F32)
     sent_ref[:, HALF:] = jnp.concatenate([gain] * N_FSDP, axis=0).astype(BF16)
-    own = jnp.broadcast_to(tok_ref[pl.ds(source + lax.rem(dev, N_FSDP), 1), :], (VIS, VIS))
+    own = jnp.broadcast_to(tok_ref[pl.ds(lax.rem(dev, N_FSDP), 1), :], (VIS, VIS))
     i, j = iota((VIS, VIS), 0), iota((VIS, VIS), 1)
     target = ((own >> 7) & (N_FSDP - 1)).astype(F32)
     mine = jnp.sum(jnp.where(i == j, target, 0.0), axis=1, keepdims=True)
@@ -138,10 +137,9 @@
 
 def program(text, vision, vision_token, gain, cotangent):
     device = jnp.full((1,), lax.axis_index(AXES), jnp.int32)
-    tokens = exchange(
-        jnp.broadcast_to(vision_token[None, :], (N_QUARTER * N_FSDP, VIS)), QUARTER + FSDP
-    )
+    asked = turned(jnp.broadcast_to(vision_token[None, :], (N_FSDP, VIS)), 1)
     rows = turned(vision, 1)
+    tokens = exchange(asked, FSDP)
 
     sent, order, taken = kernel_call(
         pack_kernel,

time: 110 us -> 108 us (0.982)
  blocking collectives: 44.3 us -> 35.7 us
  waiting for transfers between devices: 15.3 us -> 20.6 us
  starting transfers between devices: 40.2 us -> 41.7 us
    ppermute x2 -> x3, starting transfers between devices: 13.9 us -> 29.6 us  [turned(): return lax.ppermute(value, QUARTER, pairs)]
    all_to_all x2, starting transfers between devices: 26.3 us -> 12.1 us  [exchange(): return lax.all_to_all(value, axes, split_axis=0, concat_axis=0, tiled=True)]
    all_to_all x2, blocking collectives: 44.3 us -> 35.7 us  [exchange(): return lax.all_to_all(value, axes, split_axis=0, concat_axis=0, tiled=True)]
    all_to_all x2, waiting for transfers between devices: 15.3 us -> 20.6 us  [exchange(): return lax.all_to_all(value, axes, split_axis=0, concat_axis=0, tiled=True)]
  transfers between devices with their start and end apart: 4 -> 5, of which waited for: 2 -> 2; matrix products, arithmetic and copies ran while one was open for 4% -> 5% of each run, Pallas kernels for 1% -> 1%
where the time goes in v6:
time: 108 us; the launch traced here: 107 us
  starting transfers between devices  41.7 us (39%)
  blocking collectives  35.7 us (33%)
  waiting for transfers between devices  20.6 us (19%)
  other arithmetic  4.82 us (4%)
  Pallas kernels  2.7 us (2%)
    all_to_all x2, blocking collectives, exchange(): return lax.all_to_all(value, axes, split_axis=0, concat_axis=0, tiled=True)  35.7 us
    ppermute x3, starting transfers between devices, turned(): return lax.ppermute(value, QUARTER, pairs)  29.6 us
    all_to_all x2, waiting for transfers between devices, exchange(): return lax.all_to_all(value, axes, split_axis=0, concat_axis=0, tiled=True)  20.6 us
    all_to_all x2, starting transfers between devices, exchange(): return lax.all_to_all(value, axes, split_axis=0, concat_axis=0, tiled=True)  12.1 us
    reduce_sum x1, other arithmetic, program(): text_terms = jnp.sum(cotangent.astype(F32) * values * kept, axis=0)  2.34 us
  transfers between devices with their start and end apart: 5, of which 2 were waited for; matrix products, arithmetic and copies ran while one was open for 5% of the time, Pallas kernels for 1%

profile of v6, /device:TPU:1, one launch (start us, length us, event | category | flops | bytes accessed | tf_op | source)
XLA Modules:
  0.0 107.1 jit_solution(15747718333880382227)
XLA Ops:
  0.6 0.0 copy-start.1
  0.6 0.0 copy-start
  0.7 0.8 broadcast_in_dim.11
  1.5 15.7 %collective-permute-start = (s32[8,16]{1,0:T(8,128)S(1)}, s32[8,16]{1,0:T(8,128)}, u32[]{:S(2)}, u32[]{:S(2)}) collective-permute-start(s32[8,16]{1,0:T(8,128)S(1)} %broadcast_in_dim.11), channel_id=1, source_target_pairs={{0,192},{192,384},{384,576},{576,0},{1,193},{193,385},{385,577},{5... | collective-permute-start | bytes 1544 | tf_op jit(solution)/shard_map/ppermute | solution.py:131
  17.1 1.9 %collective-permute-start.1 = (bf16[16,8192]{1,0:T(8,128)(2,1)}, bf16[16,8192]{1,0:T(8,128)(2,1)S(1)}, u32[]{:S(2)}, u32[]{:S(2)}) collective-permute-start(bf16[16,8192]{1,0:T(8,128)(2,1)} %param.6), channel_id=1, source_target_pairs={{0,192},{192,384},{384,576},{576,0},{1,193},{193,385},{385,577},{5... | collective-permute-start | bytes 786440 | tf_op jit(solution)/shard_map/ppermute | solution.py:131
  19.1 2.1 %fusion.2 = f32[128]{0:T(128)S(1)} fusion(bf16[128,8192]{1,0:T(8,128)(2,1)} %param.5), kind=kLoop, calls=%fused_computation.4 | loop fusion | flops 3145600 | bytes 2097664 | tf_op jit(solution)/shard_map/reduce_sum | solution.py:153
  21.2 0.0 collective-permute-done
  21.2 8.1 %all-to-all-start = ((s32[8,1,16]{2,1,0:T(1,128)}), s32[8,1,16]{2,1,0:T(1,128)S(1)}, u32[]{:S(2)}, u32[]{:S(2)}) async-start(s32[8,1,16]{2,1,0:T(1,128)} %bitcast.2), calls=%async_computation | async-start | bytes 8192 | tf_op jit(solution)/shard_map/all_to_all | solution.py:126
  29.2 7.3 %all-to-all-done = s32[8,1,16]{2,1,0:T(1,128)S(1)} async-done(((s32[8,1,16]{2,1,0:T(1,128)}), s32[8,1,16]{2,1,0:T(1,128)S(1)}, u32[]{:S(2)}, u32[]{:S(2)}) %all-to-all-start) | async-done | bytes 544 | tf_op jit(solution)/shard_map/all_to_all | solution.py:126
  36.6 0.0 copy-done.1
  36.6 0.0 copy-done
  36.6 1.5 %shard_map.68 = (bf16[64,4224]{1,0:T(8,128)(2,1)}, bf16[32,64]{1,0:T(8,128)(2,1)S(1)}, f32[8,128]{1,0:T(8,128)S(1)}) custom-call(s32[1]{0:T(128)} %bitcast.dev_ref, s32[8,16]{1,0:T(8,128)S(1)} %bitcast.21, bf16[8,128]{1,0:T(8,128)(2,1)S(1)} %bitcast.22, bf16[128,8192]{1,0:T(8,128)(2,1)S(1)} %copy-done), custom_call_target="tpu_custom_call" | custom-call | flops 2097152 | bytes 2097152 | tf_op jit(solution)/shard_map/pallas_call | solution.py:144
  38.0 4.0 %all-to-all-start.1 = ((bf16[8,8,4224]{2,1,0:T(8,128)(2,1)}), bf16[8,8,4224]{2,1,0:T(8,128)(2,1)S(1)}, u32[]{:S(2)}, u32[]{:S(2)}) async-start(bf16[8,8,4224]{2,1,0:T(8,128)(2,1)} %bitcast.5), calls=%async_computation.1 | async-start | bytes 1081344 | tf_op jit(solution)/shard_map/all_to_all | solution.py:126
  42.1 2.3 %fusion.1 = f32[8192]{0:T(1024)S(1)} fusion(bf16[128,8192]{1,0:T(8,128)(2,1)} %param.5, bf16[128,8192]{1,0:T(8,128)(2,1)S(1)} %copy-done, f32[128]{0:T(128)S(1)} %bitcast_select_fusion), kind=kLoop, calls=%fused_computation.3 | loop fusion | flops 5234688 | bytes 4227584 | tf_op jit(solution)/shard_map/reduce_sum | solution.py:155
  44.4 0.0 collective-permute-done.1
  44.4 0.2 fusion.3
  44.6 0.1 convert_multiply_fusion.2.unit_ref
  44.8 13.2 %all-to-all-done.1 = bf16[8,8,4224]{2,1,0:T(8,128)(2,1)S(1)} async-done(((bf16[8,8,4224]{2,1,0:T(8,128)(2,1)}), bf16[8,8,4224]{2,1,0:T(8,128)(2,1)S(1)}, u32[]{:S(2)}, u32[]{:S(2)}) %all-to-all-start.1) | async-done | bytes 540704 | tf_op jit(solution)/shard_map/all_to_all | solution.py:126
  58.0 0.3 shard_map.69
  58.3 0.1 broadcast_in_dim.13.inv_ref
  58.3 0.2 shard_map.70
  58.6 12.0 %collective-permute-start.2 = (bf16[16,8192]{1,0:T(8,128)(2,1)S(1)}, bf16[16,8192]{1,0:T(8,128)(2,1)S(1)}, u32[]{:S(2)}, u32[]{:S(2)}) collective-permute-start(bf16[16,8192]{1,0:T(8,128)(2,1)S(1)} %shard_map.70), channel_id=1, source_target_pairs={{0,576},{192,0},{384,192},{576,384},{1,577},{193,1},{385,193},{577... | collective-permute-start | bytes 786440 | tf_op jit(solution)/shard_map/ppermute | solution.py:131
  70.6 15.7 %all_to_all.39 = f32[64,1,128]{2,1,0:T(1,128)S(1)} all-to-all(f32[64,1,128]{2,1,0:T(1,128)S(1)} %bitcast.20), channel_id=1, replica_groups=mesh['ylo'=2,'zhi'=2,'zlo'=6,'x'=4,'yhi'=4,'core'=2] {'yhi','core','ylo'..., dimensions={0} | all-to-all | bytes 65536 | tf_op jit(solution)/shard_map/all_to_all | solution.py:126
  86.3 0.1 reduce_sum.39
  86.4 20.0 %all_to_all.40 = f32[96,1,128]{2,1,0:T(1,128)S(1)} all-to-all(f32[96,1,128]{2,1,0:T(1,128)S(1)} %broadcast_in_dim.12), channel_id=1, replica_groups=mesh['ylo'=2,'zhi'=2,'zlo'=6,'x'=4,'yhi'=4,'core'=2] {'ylo','zhi','zlo',..., dimensions={0} | all-to-all | bytes 98304 | tf_op jit(solution)/shard_map/all_to_all | solution.py:126
  106.4 0.0 collective-permute-done.2.rows_ref
  106.4 0.7 shard_map.71
  (3 shorter events, 0.0 us)
Async XLA Ops:
  0.6 35.9 %copy-start.1 = (bf16[1024]{0:T(1024)(128)(2,1)S(1)}, bf16[1024]{0:T(1024)(128)(2,1)}, u32[]{:S(2)}) copy-start(bf16[1024]{0:T(1024)(128)(2,1)} %param.8) | copy-start | bytes 6148
  0.6 35.9 %copy-start = (bf16[128,8192]{1,0:T(8,128)(2,1)S(1)}, bf16[128,8192]{1,0:T(8,128)(2,1)}, u32[]{:S(2)}) copy-start(bf16[128,8192]{1,0:T(8,128)(2,1)} %cot_ref.1) | copy-start | bytes 6291460
  1.5 19.7 %collective-permute-start = (s32[8,16]{1,0:T(8,128)S(1)}, s32[8,16]{1,0:T(8,128)}, u32[]{:S(2)}, u32[]{:S(2)}) collective-permute-start(s32[8,16]{1,0:T(8,128)S(1)} %broadcast_in_dim.11), channel_id=1, source_target_pairs={{0,192},{192,384},{384,576},{576,0},{1,193},{193,385},{385,577},{5... | collective-permute-start | bytes 1544 | tf_op jit(solution)/shard_map/ppermute | solution.py:131
  17.1 27.3 %collective-permute-start.1 = (bf16[16,8192]{1,0:T(8,128)(2,1)}, bf16[16,8192]{1,0:T(8,128)(2,1)S(1)}, u32[]{:S(2)}, u32[]{:S(2)}) collective-permute-start(bf16[16,8192]{1,0:T(8,128)(2,1)} %param.6), channel_id=1, source_target_pairs={{0,192},{192,384},{384,576},{576,0},{1,193},{193,385},{385,577},{5... | collective-permute-start | bytes 786440 | tf_op jit(solution)/shard_map/ppermute | solution.py:131
  21.2 15.4 %all-to-all-start = ((s32[8,1,16]{2,1,0:T(1,128)}), s32[8,1,16]{2,1,0:T(1,128)S(1)}, u32[]{:S(2)}, u32[]{:S(2)}) async-start(s32[8,1,16]{2,1,0:T(1,128)} %bitcast.2), calls=%async_computation | async-start | bytes 8192 | tf_op jit(solution)/shard_map/all_to_all | solution.py:126
  38.0 20.0 %all-to-all-start.1 = ((bf16[8,8,4224]{2,1,0:T(8,128)(2,1)}), bf16[8,8,4224]{2,1,0:T(8,128)(2,1)S(1)}, u32[]{:S(2)}, u32[]{:S(2)}) async-start(bf16[8,8,4224]{2,1,0:T(8,128)(2,1)} %bitcast.5), calls=%async_computation.1 | async-start | bytes 1081344 | tf_op jit(solution)/shard_map/all_to_all | solution.py:126
  58.6 47.8 %collective-permute-start.2 = (bf16[16,8192]{1,0:T(8,128)(2,1)S(1)}, bf16[16,8192]{1,0:T(8,128)(2,1)S(1)}, u32[]{:S(2)}, u32[]{:S(2)}) collective-permute-start(bf16[16,8192]{1,0:T(8,128)(2,1)S(1)} %shard_map.70), channel_id=1, source_target_pairs={{0,576},{192,0},{384,192},{576,384},{1,577},{193,1},{385,193},{577... | collective-permute-start | bytes 786440 | tf_op jit(solution)/shard_map/ppermute | solution.py:131

commit v7 on v5

--- a/solution.py
+++ b/solution.py
@@ -7,7 +7,7 @@
 
 AXES = ("ylo", "zhi", "zlo", "x", "yhi", "core")
 QUARTER = ("ylo", "zhi")
-GRP = ("ylo", "zhi", "zlo", "x")
+ZX = ("zhi", "zlo", "x")
 FSDP = ("yhi", "core")
 PLANE = ("yhi", "core", "ylo", "x")
 SIZES = (2, 2, 6, 4, 4, 2)
@@ -85,7 +85,9 @@
         total = jnp.sum(product, axis=0, keepdims=True)
         block = k // LANES
         rows = [total[:, b * LANES : (b + 1) * LANES] for b in range(8)]
-        terms_ref[block : block + 8, :] = text_ref[block : block + 8, :] + jnp.concatenate(rows, axis=0)
+        rows = text_ref[block : block + 8, :] + jnp.concatenate(rows, axis=0)
+        terms_ref[2 * block : 2 * block + 8, :] = rows
+        terms_ref[2 * block + 8 : 2 * block + 16, :] = rows
 
 
 def grads_kernel(arrived_ref, upper_ref, unit_ref, inv_ref, grad_ref):
@@ -105,11 +107,10 @@
 
 def finish_kernel(parts_ref, rows_ref, grad_ref, sum_ref):
     grad_ref[...] = rows_ref[...]
-    for low in range(2):
-        total = parts_ref[low * 48 : low * 48 + 4, :]
-        for z in range(1, 12):
-            total = total + parts_ref[low * 48 + 4 * z : low * 48 + 4 * z + 4, :]
-        sum_ref[4 * low : 4 * low + 4, :] = total
+    total = parts_ref[:8, :]
+    for z in range(1, 12):
+        total = total + parts_ref[8 * z : 8 * z + 8, :]
+    sum_ref[...] = total
 
 
 def kernel_call(body, outs, in_specs, cost):
@@ -160,7 +161,7 @@
     inv_v = lax.rsqrt(jnp.mean(values_v * values_v, axis=-1, keepdims=True) + 1e-06)
     unit = values_v * inv_v
     terms, upper = kernel_call(
-        terms_kernel, [shape(BLOCKS, LANES), shape(VIS, WIDTH, dtype=BF16)], [VMEM] * 4, 2**20
+        terms_kernel, [shape(2 * BLOCKS, LANES), shape(VIS, WIDTH, dtype=BF16)], [VMEM] * 4, 2**20
     )(order, arrived, unit, text_terms.reshape(BLOCKS, LANES))
     (grad,) = kernel_call(grads_kernel, [shape(VIS, WIDTH, dtype=BF16)], [VMEM] * 4, 2**20)(
         arrived, upper, unit, jnp.broadcast_to(inv_v, (VIS, LANES))
@@ -168,8 +169,8 @@
     vision_grad = turned(grad, -1)
 
     pieces = exchange(terms, PLANE)
-    part = jnp.sum(pieces, axis=0)
-    parts = exchange(jnp.broadcast_to(part[None, :], (DEVICES // N_FSDP, LANES)), GRP)
+    part = jnp.sum(pieces.reshape(64, 2, LANES), axis=0)
+    parts = exchange(jnp.broadcast_to(part[None], (48, 2, LANES)).reshape(96, LANES), ZX)
     vision_grad, gain_grad = kernel_call(
         finish_kernel, [shape(VIS, WIDTH, dtype=BF16), shape(8, LANES)], [VMEM] * 2, 2**19
     )(parts, vision_grad)

time: 110 us -> 104 us (0.945)
  blocking collectives: 44.3 us -> 0 us
  starting transfers between devices: 40.2 us -> 60.2 us
  waiting for transfers between devices: 15.3 us -> 32.2 us
    all_to_all x2 -> x0, blocking collectives: 44.3 us -> none  [exchange(): return lax.all_to_all(value, axes, split_axis=0, concat_axis=0, tiled=True)]
    all_to_all x2 -> x4, starting transfers between devices: 26.3 us -> 47.3 us  [exchange(): return lax.all_to_all(value, axes, split_axis=0, concat_axis=0, tiled=True)]
    all_to_all x2 -> x4, waiting for transfers between devices: 15.3 us -> 32.2 us  [exchange(): return lax.all_to_all(value, axes, split_axis=0, concat_axis=0, tiled=True)]
  transfers between devices with their start and end apart: 4 -> 6, of which waited for: 2 -> 4; matrix products, arithmetic and copies ran while one was open for 4% -> 5% of each run, Pallas kernels for 1% -> 2%
where the time goes in v7:
time: 104 us; the launch traced here: 103 us
  starting transfers between devices  60.2 us (58%)
  waiting for transfers between devices  32.2 us (31%)
  other arithmetic  4.81 us (5%)
  Pallas kernels  3.36 us (3%)
  local copies, waits for them, and re-layouts  2.13 us (2%)
    all_to_all x4, starting transfers between devices, exchange(): return lax.all_to_all(value, axes, split_axis=0, concat_axis=0, tiled=True)  47.3 us
    all_to_all x4, waiting for transfers between devices, exchange(): return lax.all_to_all(value, axes, split_axis=0, concat_axis=0, tiled=True)  32.2 us
    ppermute x2, starting transfers between devices, turned(): return lax.ppermute(value, QUARTER, pairs)  12.9 us
    reduce_sum x1, other arithmetic, program(): text_terms = jnp.sum(cotangent.astype(F32) * values * kept, axis=0)  2.34 us
  transfers between devices with their start and end apart: 6, of which 4 were waited for; matrix products, arithmetic and copies ran while one was open for 5% of the time, Pallas kernels for 2%

profile of v7, /device:TPU:1, one launch (start us, length us, event | category | flops | bytes accessed | tf_op | source)
XLA Modules:
  0.0 103.5 jit_solution(18119629136804124547)
XLA Ops:
  0.6 0.0 copy-start.1
  0.6 0.0 copy-start
  0.7 1.4 %broadcast_in_dim.11 = s32[32,1,16]{2,1,0:T(1,128)} broadcast(s32[16]{0:T(128)} %param.7), dimensions={2} | broadcast | bytes 2112 | tf_op jit(solution)/shard_map/broadcast_in_dim | solution.py:143
  2.1 21.4 %all-to-all-start = ((s32[32,1,16]{2,1,0:T(1,128)}), s32[32,1,16]{2,1,0:T(1,128)S(1)}, u32[]{:S(2)}, u32[]{:S(2)}) async-start(s32[32,1,16]{2,1,0:T(1,128)} %broadcast_in_dim.11), calls=%async_computation | async-start | bytes 32768 | tf_op jit(solution)/shard_map/all_to_all | solution.py:128
  23.5 9.6 %collective-permute-start = (bf16[16,8192]{1,0:T(8,128)(2,1)}, bf16[16,8192]{1,0:T(8,128)(2,1)S(1)}, u32[]{:S(2)}, u32[]{:S(2)}) collective-permute-start(bf16[16,8192]{1,0:T(8,128)(2,1)} %param.6), channel_id=1, source_target_pairs={{0,192},{192,384},{384,576},{576,0},{1,193},{193,385},{385,577},{5... | collective-permute-start | bytes 786440 | tf_op jit(solution)/shard_map/ppermute | solution.py:133
  33.1 2.1 %fusion.2 = f32[128]{0:T(128)S(1)} fusion(bf16[128,8192]{1,0:T(8,128)(2,1)} %param.5), kind=kLoop, calls=%fused_computation.4 | loop fusion | flops 3145600 | bytes 2097664 | tf_op jit(solution)/shard_map/reduce_sum | solution.py:156
  35.2 2.4 %all-to-all-done = s32[32,1,16]{2,1,0:T(1,128)S(1)} async-done(((s32[32,1,16]{2,1,0:T(1,128)}), s32[32,1,16]{2,1,0:T(1,128)S(1)}, u32[]{:S(2)}, u32[]{:S(2)}) %all-to-all-start) | async-done | bytes 2080 | tf_op jit(solution)/shard_map/all_to_all | solution.py:128
  37.6 0.0 copy-done.1
  37.6 0.0 copy-done
  37.6 1.5 %shard_map.68 = (bf16[64,4224]{1,0:T(8,128)(2,1)}, bf16[32,64]{1,0:T(8,128)(2,1)S(1)}, f32[8,128]{1,0:T(8,128)S(1)}) custom-call(s32[1]{0:T(128)} %bitcast.dev_ref, s32[32,16]{1,0:T(8,128)S(1)} %bitcast.15, bf16[8,128]{1,0:T(8,128)(2,1)S(1)} %bitcast.16, bf16[128,8192]{1,0:T(8,128)(2,1)S(1)} %copy-done), custom_call_target="tpu_custom_call" | custom-call | flops 2097152 | bytes 2097152 | tf_op jit(solution)/shard_map/pallas_call | solution.py:147
  39.1 4.9 %all-to-all-start.1 = ((bf16[8,8,4224]{2,1,0:T(8,128)(2,1)}), bf16[8,8,4224]{2,1,0:T(8,128)(2,1)S(1)}, u32[]{:S(2)}, u32[]{:S(2)}) async-start(bf16[8,8,4224]{2,1,0:T(8,128)(2,1)} %bitcast.3), calls=%async_computation.1 | async-start | bytes 1081344 | tf_op jit(solution)/shard_map/all_to_all | solution.py:128
  44.0 2.3 %fusion.1 = f32[8192]{0:T(1024)S(1)} fusion(bf16[128,8192]{1,0:T(8,128)(2,1)} %param.5, bf16[128,8192]{1,0:T(8,128)(2,1)S(1)} %copy-done, f32[128]{0:T(128)S(1)} %bitcast_select_fusion), kind=kLoop, calls=%fused_computation.3 | loop fusion | flops 5234688 | bytes 4227584 | tf_op jit(solution)/shard_map/reduce_sum | solution.py:158
  46.4 0.0 collective-permute-done
  46.4 0.2 fusion.3
  46.6 0.1 convert_multiply_fusion.2.unit_ref
  46.7 12.9 %all-to-all-done.1 = bf16[8,8,4224]{2,1,0:T(8,128)(2,1)S(1)} async-done(((bf16[8,8,4224]{2,1,0:T(8,128)(2,1)}), bf16[8,8,4224]{2,1,0:T(8,128)(2,1)S(1)}, u32[]{:S(2)}, u32[]{:S(2)}) %all-to-all-start.1) | async-done | bytes 540704 | tf_op jit(solution)/shard_map/all_to_all | solution.py:128
  59.6 0.9 shard_map.69
  60.5 8.0 %all-to-all-start.2 = ((f32[64,2,128]{2,1,0:T(2,128)}), f32[64,2,128]{2,1,0:T(2,128)S(1)}, u32[]{:S(2)}, u32[]{:S(2)}) async-start(f32[64,2,128]{2,1,0:T(2,128)} %bitcast.7), calls=%async_computation.2 | async-start | bytes 131072 | tf_op jit(solution)/shard_map/all_to_all | solution.py:128
  68.5 0.1 broadcast_in_dim.13.inv_ref
  68.6 0.2 shard_map.70
  68.8 3.3 %collective-permute-start.1 = (bf16[16,8192]{1,0:T(8,128)(2,1)S(1)}, bf16[16,8192]{1,0:T(8,128)(2,1)S(1)}, u32[]{:S(2)}, u32[]{:S(2)}) collective-permute-start(bf16[16,8192]{1,0:T(8,128)(2,1)S(1)} %shard_map.70), channel_id=1, source_target_pairs={{0,576},{192,0},{384,192},{576,384},{1,577},{193,1},{385,193},{577... | collective-permute-start | bytes 786440 | tf_op jit(solution)/shard_map/ppermute | solution.py:133
  72.2 5.7 %all-to-all-done.2 = f32[64,2,128]{2,1,0:T(2,128)S(1)} async-done(((f32[64,2,128]{2,1,0:T(2,128)}), f32[64,2,128]{2,1,0:T(2,128)S(1)}, u32[]{:S(2)}, u32[]{:S(2)}) %all-to-all-start.2) | async-done | bytes 65568 | tf_op jit(solution)/shard_map/all_to_all | solution.py:128
  77.9 0.1 reduce_sum.39
  78.0 0.6 broadcast_in_dim.12
  78.6 13.0 %all-to-all-start.3 = ((f32[48,2,128]{2,1,0:T(2,128)}), f32[48,2,128]{2,1,0:T(2,128)S(1)}, u32[]{:S(2)}, u32[]{:S(2)}) async-start(f32[48,2,128]{2,1,0:T(2,128)} %broadcast_in_dim.12), calls=%async_computation.3 | async-start | bytes 98304 | tf_op jit(solution)/shard_map/all_to_all | solution.py:128
  91.6 0.0 collective-permute-done.1.rows_ref
  91.6 11.2 %all-to-all-done.3 = f32[48,2,128]{2,1,0:T(2,128)S(1)} async-done(((f32[48,2,128]{2,1,0:T(2,128)}), f32[48,2,128]{2,1,0:T(2,128)S(1)}, u32[]{:S(2)}, u32[]{:S(2)}) %all-to-all-start.3) | async-done | bytes 49184 | tf_op jit(solution)/shard_map/all_to_all | solution.py:128
  102.7 0.7 shard_map.71
  (2 shorter events, 0.0 us)
Async XLA Ops:
  0.6 37.0 %copy-start.1 = (bf16[1024]{0:T(1024)(128)(2,1)S(1)}, bf16[1024]{0:T(1024)(128)(2,1)}, u32[]{:S(2)}) copy-start(bf16[1024]{0:T(1024)(128)(2,1)} %param.8) | copy-start | bytes 6148
  0.6 37.0 %copy-start = (bf16[128,8192]{1,0:T(8,128)(2,1)S(1)}, bf16[128,8192]{1,0:T(8,128)(2,1)}, u32[]{:S(2)}) copy-start(bf16[128,8192]{1,0:T(8,128)(2,1)} %cot_ref.1) | copy-start | bytes 6291460
  2.1 35.5 %all-to-all-start = ((s32[32,1,16]{2,1,0:T(1,128)}), s32[32,1,16]{2,1,0:T(1,128)S(1)}, u32[]{:S(2)}, u32[]{:S(2)}) async-start(s32[32,1,16]{2,1,0:T(1,128)} %broadcast_in_dim.11), calls=%async_computation | async-start | bytes 32768 | tf_op jit(solution)/shard_map/all_to_all | solution.py:128
  23.5 22.9 %collective-permute-start = (bf16[16,8192]{1,0:T(8,128)(2,1)}, bf16[16,8192]{1,0:T(8,128)(2,1)S(1)}, u32[]{:S(2)}, u32[]{:S(2)}) collective-permute-start(bf16[16,8192]{1,0:T(8,128)(2,1)} %param.6), channel_id=1, source_target_pairs={{0,192},{192,384},{384,576},{576,0},{1,193},{193,385},{385,577},{5... | collective-permute-start | bytes 786440 | tf_op jit(solution)/shard_map/ppermute | solution.py:133
  39.1 20.5 %all-to-all-start.1 = ((bf16[8,8,4224]{2,1,0:T(8,128)(2,1)}), bf16[8,8,4224]{2,1,0:T(8,128)(2,1)S(1)}, u32[]{:S(2)}, u32[]{:S(2)}) async-start(bf16[8,8,4224]{2,1,0:T(8,128)(2,1)} %bitcast.3), calls=%async_computation.1 | async-start | bytes 1081344 | tf_op jit(solution)/shard_map/all_to_all | solution.py:128
  60.5 17.4 %all-to-all-start.2 = ((f32[64,2,128]{2,1,0:T(2,128)}), f32[64,2,128]{2,1,0:T(2,128)S(1)}, u32[]{:S(2)}, u32[]{:S(2)}) async-start(f32[64,2,128]{2,1,0:T(2,128)} %bitcast.7), calls=%async_computation.2 | async-start | bytes 131072 | tf_op jit(solution)/shard_map/all_to_all | solution.py:128
  68.8 22.7 %collective-permute-start.1 = (bf16[16,8192]{1,0:T(8,128)(2,1)S(1)}, bf16[16,8192]{1,0:T(8,128)(2,1)S(1)}, u32[]{:S(2)}, u32[]{:S(2)}) collective-permute-start(bf16[16,8192]{1,0:T(8,128)(2,1)S(1)} %shard_map.70), channel_id=1, source_target_pairs={{0,576},{192,0},{384,192},{576,384},{1,577},{193,1},{385,193},{577... | collective-permute-start | bytes 786440 | tf_op jit(solution)/shard_map/ppermute | solution.py:133
  78.6 24.1 %all-to-all-start.3 = ((f32[48,2,128]{2,1,0:T(2,128)}), f32[48,2,128]{2,1,0:T(2,128)S(1)}, u32[]{:S(2)}, u32[]{:S(2)}) async-start(f32[48,2,128]{2,1,0:T(2,128)} %broadcast_in_dim.12), calls=%async_computation.3 | async-start | bytes 98304 | tf_op jit(solution)/shard_map/all_to_all | solution.py:128

commit v8 on v7

--- a/solution.py
+++ b/solution.py
@@ -105,20 +105,33 @@
         grad_ref[:, at] = (inv * (scaled - unit_ref[:, at] * inner)).astype(BF16)
 
 
-def finish_kernel(parts_ref, rows_ref, grad_ref, sum_ref):
-    grad_ref[...] = rows_ref[...]
+def repeat_kernel(pieces_ref, parts_ref):
+    total = pieces_ref[:8, :]
+    for k in range(8, 2 * BLOCKS, 8):
+        total = total + pieces_ref[k : k + 8, :]
+    total = total + pltpu.roll(total, 4, 0)
+    total = total + pltpu.roll(total, 2, 0)
+    for k in range(0, 96, 8):
+        parts_ref[k : k + 8, :] = total
+
+
+def finish_kernel(parts_ref, rows_ref, grad_ref, sum_ref, sem):
+    copy = pltpu.make_async_copy(rows_ref, grad_ref, sem)
+    copy.start()
     total = parts_ref[:8, :]
     for z in range(1, 12):
         total = total + parts_ref[8 * z : 8 * z + 8, :]
     sum_ref[...] = total
-
-
-def kernel_call(body, outs, in_specs, cost):
+    copy.wait()
+
+
+def kernel_call(body, outs, in_specs, cost, out_specs=None, scratch=()):
     return pl.pallas_call(
         body,
         out_shape=outs,
         in_specs=in_specs,
-        out_specs=[VMEM] * len(outs),
+        out_specs=out_specs or [VMEM] * len(outs),
+        scratch_shapes=scratch,
         compiler_params=pltpu.CompilerParams(vmem_limit_bytes=16 * 2**20),
         cost_estimate=pl.CostEstimate(flops=cost, bytes_accessed=cost, transcendentals=0),
     )
@@ -169,10 +182,11 @@
     vision_grad = turned(grad, -1)
 
     pieces = exchange(terms, PLANE)
-    part = jnp.sum(pieces.reshape(64, 2, LANES), axis=0)
-    parts = exchange(jnp.broadcast_to(part[None], (48, 2, LANES)).reshape(96, LANES), ZX)
+    (part,) = kernel_call(repeat_kernel, [shape(96, LANES)], [VMEM], 2**16)(pieces)
+    parts = exchange(part, ZX)
     vision_grad, gain_grad = kernel_call(
-        finish_kernel, [shape(VIS, WIDTH, dtype=BF16), shape(8, LANES)], [VMEM] * 2, 2**19
+        finish_kernel, [shape(VIS, WIDTH, dtype=BF16), shape(8, LANES)], [VMEM] * 2, 2**19,
+        [pl.BlockSpec(memory_space=pl.ANY), VMEM], [pltpu.SemaphoreType.DMA]
     )(parts, vision_grad)
     return (vision_grad, gain_grad.reshape(WIDTH // N_FSDP))
 

time: 104 us -> 104 us (level)
  Pallas kernels: 3.36 us -> 4.58 us
where the time goes in v8:
time: 104 us
  starting transfers between devices  60.2 us (58%)
  waiting for transfers between devices  32.2 us (31%)
  other arithmetic  4.73 us (5%)
  Pallas kernels  4.58 us (4%)
  local copies, waits for them, and re-layouts  1.5 us (1%)
    all_to_all x4, starting transfers between devices, exchange(): return lax.all_to_all(value, axes, split_axis=0, concat_axis=0, tiled=True)  47.3 us
    all_to_all x4, waiting for transfers between devices, exchange(): return lax.all_to_all(value, axes, split_axis=0, concat_axis=0, tiled=True)  32.2 us
    ppermute x2, starting transfers between devices, turned(): return lax.ppermute(value, QUARTER, pairs)  12.9 us
    reduce_sum x1, other arithmetic, program(): text_terms = jnp.sum(cotangent.astype(F32) * values * kept, axis=0)  2.34 us
  transfers between devices with their start and end apart: 6, of which 4 were waited for; matrix products, arithmetic and copies ran while one was open for 5% of the time, Pallas kernels for 2%

profile of v8, /device:TPU:1, one launch (start us, length us, event | category | flops | bytes accessed | tf_op | source)
XLA Modules:
  0.0 104.0 jit_solution(4342350068912497869)
XLA Ops:
  0.6 0.0 copy-start.1
  0.6 0.0 copy-start
  0.7 1.4 %broadcast_in_dim.9 = s32[32,1,16]{2,1,0:T(1,128)} broadcast(s32[16]{0:T(128)} %param.7), dimensions={2} | broadcast | bytes 2112 | tf_op jit(solution)/shard_map/broadcast_in_dim | solution.py:156
  2.1 21.4 %all-to-all-start = ((s32[32,1,16]{2,1,0:T(1,128)}), s32[32,1,16]{2,1,0:T(1,128)S(1)}, u32[]{:S(2)}, u32[]{:S(2)}) async-start(s32[32,1,16]{2,1,0:T(1,128)} %broadcast_in_dim.9), calls=%async_computation | async-start | bytes 32768 | tf_op jit(solution)/shard_map/all_to_all | solution.py:141
  23.5 9.6 %collective-permute-start = (bf16[16,8192]{1,0:T(8,128)(2,1)}, bf16[16,8192]{1,0:T(8,128)(2,1)S(1)}, u32[]{:S(2)}, u32[]{:S(2)}) collective-permute-start(bf16[16,8192]{1,0:T(8,128)(2,1)} %param.6), channel_id=1, source_target_pairs={{0,192},{192,384},{384,576},{576,0},{1,193},{193,385},{385,577},{5... | collective-permute-start | bytes 786440 | tf_op jit(solution)/shard_map/ppermute | solution.py:146
  33.1 2.1 %fusion.2 = f32[128]{0:T(128)S(1)} fusion(bf16[128,8192]{1,0:T(8,128)(2,1)} %param.5), kind=kLoop, calls=%fused_computation.4 | loop fusion | flops 3145600 | bytes 2097664 | tf_op jit(solution)/shard_map/reduce_sum | solution.py:169
  35.2 2.4 %all-to-all-done = s32[32,1,16]{2,1,0:T(1,128)S(1)} async-done(((s32[32,1,16]{2,1,0:T(1,128)}), s32[32,1,16]{2,1,0:T(1,128)S(1)}, u32[]{:S(2)}, u32[]{:S(2)}) %all-to-all-start) | async-done | bytes 2080 | tf_op jit(solution)/shard_map/all_to_all | solution.py:141
  37.6 0.0 copy-done.1
  37.6 0.0 copy-done
  37.6 1.5 %shard_map.68 = (bf16[64,4224]{1,0:T(8,128)(2,1)}, bf16[32,64]{1,0:T(8,128)(2,1)S(1)}, f32[8,128]{1,0:T(8,128)S(1)}) custom-call(s32[1]{0:T(128)} %bitcast.dev_ref, s32[32,16]{1,0:T(8,128)S(1)} %bitcast.18, bf16[8,128]{1,0:T(8,128)(2,1)S(1)} %bitcast.19, bf16[128,8192]{1,0:T(8,128)(2,1)S(1)} %copy-done), custom_call_target="tpu_custom_call" | custom-call | flops 2097152 | bytes 2097152 | tf_op jit(solution)/shard_map/pallas_call | solution.py:160
  39.1 4.9 %all-to-all-start.1 = ((bf16[8,8,4224]{2,1,0:T(8,128)(2,1)}), bf16[8,8,4224]{2,1,0:T(8,128)(2,1)S(1)}, u32[]{:S(2)}, u32[]{:S(2)}) async-start(bf16[8,8,4224]{2,1,0:T(8,128)(2,1)} %bitcast.3), calls=%async_computation.1 | async-start | bytes 1081344 | tf_op jit(solution)/shard_map/all_to_all | solution.py:141
  44.0 2.3 %fusion.1 = f32[8192]{0:T(1024)S(1)} fusion(bf16[128,8192]{1,0:T(8,128)(2,1)} %param.5, bf16[128,8192]{1,0:T(8,128)(2,1)S(1)} %copy-done, f32[128]{0:T(128)S(1)} %bitcast_select_fusion), kind=kLoop, calls=%fused_computation.3 | loop fusion | flops 5234688 | bytes 4227584 | tf_op jit(solution)/shard_map/reduce_sum | solution.py:171
  46.4 0.0 collective-permute-done
  46.4 0.2 fusion.3
  46.6 0.1 convert_multiply_fusion.2.unit_ref
  46.7 12.9 %all-to-all-done.1 = bf16[8,8,4224]{2,1,0:T(8,128)(2,1)S(1)} async-done(((bf16[8,8,4224]{2,1,0:T(8,128)(2,1)}), bf16[8,8,4224]{2,1,0:T(8,128)(2,1)S(1)}, u32[]{:S(2)}, u32[]{:S(2)}) %all-to-all-start.1) | async-done | bytes 540704 | tf_op jit(solution)/shard_map/all_to_all | solution.py:141
  59.6 0.9 shard_map.69
  60.5 8.0 %all-to-all-start.2 = ((f32[64,2,128]{2,1,0:T(2,128)}), f32[64,2,128]{2,1,0:T(2,128)S(1)}, u32[]{:S(2)}, u32[]{:S(2)}) async-start(f32[64,2,128]{2,1,0:T(2,128)} %bitcast.7), calls=%async_computation.2 | async-start | bytes 131072 | tf_op jit(solution)/shard_map/all_to_all | solution.py:141
  68.5 0.1 broadcast_in_dim.10.inv_ref
  68.6 0.2 shard_map.71
  68.8 3.3 %collective-permute-start.1 = (bf16[16,8192]{1,0:T(8,128)(2,1)S(1)}, bf16[16,8192]{1,0:T(8,128)(2,1)S(1)}, u32[]{:S(2)}, u32[]{:S(2)}) collective-permute-start(bf16[16,8192]{1,0:T(8,128)(2,1)S(1)} %shard_map.71), channel_id=1, source_target_pairs={{0,576},{192,0},{384,192},{576,384},{1,577},{193,1},{385,193},{577... | collective-permute-start | bytes 786440 | tf_op jit(solution)/shard_map/ppermute | solution.py:146
  72.2 5.7 %all-to-all-done.2 = f32[64,2,128]{2,1,0:T(2,128)S(1)} async-done(((f32[64,2,128]{2,1,0:T(2,128)}), f32[64,2,128]{2,1,0:T(2,128)S(1)}, u32[]{:S(2)}, u32[]{:S(2)}) %all-to-all-start.2) | async-done | bytes 65568 | tf_op jit(solution)/shard_map/all_to_all | solution.py:141
  77.9 0.6 shard_map.70
  78.5 13.0 %all-to-all-start.3 = ((f32[48,2,128]{2,1,0:T(2,128)}), f32[48,2,128]{2,1,0:T(2,128)S(1)}, u32[]{:S(2)}, u32[]{:S(2)}) async-start(f32[48,2,128]{2,1,0:T(2,128)} %bitcast.9), calls=%async_computation.3 | async-start | bytes 98304 | tf_op jit(solution)/shard_map/all_to_all | solution.py:141
  91.5 0.0 collective-permute-done.1.rows_ref
  91.5 11.2 %all-to-all-done.3 = f32[48,2,128]{2,1,0:T(2,128)S(1)} async-done(((f32[48,2,128]{2,1,0:T(2,128)}), f32[48,2,128]{2,1,0:T(2,128)S(1)}, u32[]{:S(2)}, u32[]{:S(2)}) %all-to-all-start.3) | async-done | bytes 49184 | tf_op jit(solution)/shard_map/all_to_all | solution.py:141
  102.7 1.3 %shard_map.72 = (bf16[16,8192]{1,0:T(8,128)(2,1)}, f32[8,128]{1,0:T(8,128)}) custom-call(f32[96,128]{1,0:T(8,128)S(1)} %bitcast.16, bf16[16,8192]{1,0:T(8,128)(2,1)S(1)} %collective-permute-done.1.rows_ref), custom_call_target="tpu_custom_call" | custom-call | flops 524288 | bytes 524288 | tf_op jit(solution)/shard_map/pallas_call | solution.py:187
  (2 shorter events, 0.0 us)
Async XLA Ops:
  0.6 37.0 %copy-start.1 = (bf16[1024]{0:T(1024)(128)(2,1)S(1)}, bf16[1024]{0:T(1024)(128)(2,1)}, u32[]{:S(2)}) copy-start(bf16[1024]{0:T(1024)(128)(2,1)} %param.8) | copy-start | bytes 6148
  0.6 37.0 %copy-start = (bf16[128,8192]{1,0:T(8,128)(2,1)S(1)}, bf16[128,8192]{1,0:T(8,128)(2,1)}, u32[]{:S(2)}) copy-start(bf16[128,8192]{1,0:T(8,128)(2,1)} %cot_ref.1) | copy-start | bytes 6291460
  2.1 35.5 %all-to-all-start = ((s32[32,1,16]{2,1,0:T(1,128)}), s32[32,1,16]{2,1,0:T(1,128)S(1)}, u32[]{:S(2)}, u32[]{:S(2)}) async-start(s32[32,1,16]{2,1,0:T(1,128)} %broadcast_in_dim.9), calls=%async_computation | async-start | bytes 32768 | tf_op jit(solution)/shard_map/all_to_all | solution.py:141
  23.5 22.9 %collective-permute-start = (bf16[16,8192]{1,0:T(8,128)(2,1)}, bf16[16,8192]{1,0:T(8,128)(2,1)S(1)}, u32[]{:S(2)}, u32[]{:S(2)}) collective-permute-start(bf16[16,8192]{1,0:T(8,128)(2,1)} %param.6), channel_id=1, source_target_pairs={{0,192},{192,384},{384,576},{576,0},{1,193},{193,385},{385,577},{5... | collective-permute-start | bytes 786440 | tf_op jit(solution)/shard_map/ppermute | solution.py:146
  39.1 20.5 %all-to-all-start.1 = ((bf16[8,8,4224]{2,1,0:T(8,128)(2,1)}), bf16[8,8,4224]{2,1,0:T(8,128)(2,1)S(1)}, u32[]{:S(2)}, u32[]{:S(2)}) async-start(bf16[8,8,4224]{2,1,0:T(8,128)(2,1)} %bitcast.3), calls=%async_computation.1 | async-start | bytes 1081344 | tf_op jit(solution)/shard_map/all_to_all | solution.py:141
  60.5 17.4 %all-to-all-start.2 = ((f32[64,2,128]{2,1,0:T(2,128)}), f32[64,2,128]{2,1,0:T(2,128)S(1)}, u32[]{:S(2)}, u32[]{:S(2)}) async-start(f32[64,2,128]{2,1,0:T(2,128)} %bitcast.7), calls=%async_computation.2 | async-start | bytes 131072 | tf_op jit(solution)/shard_map/all_to_all | solution.py:141
  68.8 22.7 %collective-permute-start.1 = (bf16[16,8192]{1,0:T(8,128)(2,1)S(1)}, bf16[16,8192]{1,0:T(8,128)(2,1)S(1)}, u32[]{:S(2)}, u32[]{:S(2)}) collective-permute-start(bf16[16,8192]{1,0:T(8,128)(2,1)S(1)} %shard_map.71), channel_id=1, source_target_pairs={{0,576},{192,0},{384,192},{576,384},{1,577},{193,1},{385,193},{577... | collective-permute-start | bytes 786440 | tf_op jit(solution)/shard_map/ppermute | solution.py:146
  78.5 24.1 %all-to-all-start.3 = ((f32[48,2,128]{2,1,0:T(2,128)}), f32[48,2,128]{2,1,0:T(2,128)S(1)}, u32[]{:S(2)}, u32[]{:S(2)}) async-start(f32[48,2,128]{2,1,0:T(2,128)} %bitcast.9), calls=%async_computation.3 | async-start | bytes 98304 | tf_op jit(solution)/shard_map/all_to_all | solution.py:141
